TPU v7x, 128 devices: a whole 4x4x4 slice. The times are simulated.
128 devices in a mesh: rows: 128 (over y, x, z, core).
Axes of the slice: x: 4, y: 4, z: 4, core: 2. Of those that a mesh axis runs over, the one named last changes fastest.
Arguments:
- left: bfloat16 [524288, 512], P('rows'), may hold values from -24 to 24
- right: bfloat16 [524288, 512], P('rows'), may hold values from -6 to 6
- tiles: bfloat16 [2, 64, 128, 128], replicated, may hold values from -0.1875 to 0.1875
- source_blocks: int32 [2, 4096, 16], P(None, 'rows'), may hold values from 0 to 287, as said below
- tile_index: int32 [2, 4096, 16], P(None, 'rows'), may hold values from -1 to 63
- send_blocks: int32 [16384, 2], P('rows'), may hold values from -1 to 31, as said below
Outputs:
- moments: float32 [2, 512, 512], P(None, 'rows')
Inputs may be any that keep to these rules, and one draw needn't show every extreme that they name: `source_blocks`: every slot with v >= 32 names a slot of send_blocks that is not -1. Empty slots (tile -1) name an own block. Each provided block is named by some slot of the receiving device. Some device receives 2 blocks from every device, and some device has all of its slots filled. `send_blocks`: slot 0 is never -1; the two blocks that one device provides to another are different.
All inputs are finite; a program needn't handle non-finite values.
Results may differ from a plain program's by a relative error of at most 0.0029.
Values may be sent and summed in bfloat16 or wider, within the bound.
A program may use at most 192 MiB of HBM per device.

v0:
```python
import math

import jax
import jax.numpy as jnp
from jax import lax
from jax.sharding import PartitionSpec as P


def gather_group(source_pool, tile_table, group_sources, group_tiles):
    live = (group_tiles >= 0)[..., None, None]
    chosen = jnp.where(live, tile_table[jnp.maximum(group_tiles, 0)], jnp.zeros((), jnp.bfloat16))
    picked = source_pool[group_sources]
    return jnp.einsum("bkij,bkjn->bin", chosen, picked, preferred_element_type=jnp.float32)


def apply_current(source_pool, tile_table, sources, indices, local_blocks):
    slot_count = sources.shape[-1]
    group_size = math.gcd(local_blocks, 8)

    def one_group(operands):
        return gather_group(source_pool, tile_table, operands[0], operands[1])

    result = lax.map(
        one_group,
        (sources.reshape(-1, group_size, slot_count), indices.reshape(-1, group_size, slot_count)),
    )
    return result.reshape(local_blocks * source_pool.shape[1], source_pool.shape[2])


def fetch_blocks(blocks, send_blocks):
    opened = (send_blocks >= 0)[..., None, None]
    outgoing = jnp.where(opened, blocks[jnp.maximum(send_blocks, 0)], jnp.zeros((), jnp.bfloat16))
    arrived = lax.all_to_all(outgoing, "rows", split_axis=0, concat_axis=0, tiled=True)
    return arrived.reshape(-1, blocks.shape[1], blocks.shape[2])


def body(left, right, tiles, source_blocks, tile_index, send_blocks):
    block_rows = tiles.shape[-1]
    vectors = right.shape[1]
    local_blocks = right.shape[0] // block_rows
    devices = lax.axis_size("rows")
    blocks = right.reshape(local_blocks, block_rows, vectors)
    norm_scale = 1.0 / math.sqrt(local_blocks * block_rows * devices)
    currents = []
    arrived = fetch_blocks(blocks, send_blocks)
    source_pool = jnp.concatenate([blocks, arrived], axis=0)
    for direction in range(2):
        whole_part = apply_current(
            source_pool,
            tiles[direction],
            source_blocks[direction],
            tile_index[direction],
            local_blocks,
        )
        currents.append(whole_part.astype(jnp.bfloat16))
    pieces = []
    for direction in range(2):
        product = lax.dot_general(
            left, currents[direction], (((0,), (0,)), ((), ())), preferred_element_type=jnp.float32
        )
        pieces.append(
            lax.psum_scatter(product * norm_scale, "rows", scatter_dimension=0, tiled=True)
        )
    return jnp.stack(pieces)


def solution(mesh):
    placed = (
        P("rows", None),
        P("rows", None),
        P(),
        P(None, "rows", None),
        P(None, "rows", None),
        P("rows", None),
    )
    return jax.shard_map(
        body, mesh=mesh, in_specs=placed, out_specs=P(None, "rows", None), check_vma=False
    )
```

profile of v0, /device:TPU:1, one launch (start us, length us, event | category | flops | bytes accessed | tf_op | source)
XLA Modules:
  0.0 1013.5 jit_solution(294551788289210130)
XLA Ops:
  8.3 16.1 %gather_fusion.4 = bf16[256,128,512]{2,1,0:T(8,128)(2,1)} fusion(bf16[32,128,512]{2,1,0:T(8,128)(2,1)} %bitcast.83, s32[1024]{0:T(1024)S(1)} %pad_clamp_fusion.4), kind=kCustom, calls=%fused_computation.4 | custom fusion | bytes 67109888 | tf_op jit(solution)/shard_map/gather | solution.py:32
  24.4 22.7 %broadcast_select_fusion = bf16[128,2,128,512]{3,2,1,0:T(8,128)(2,1)} fusion(bf16[128,2,128,512]{3,2,1,0:T(8,128)(2,1)} %bitcast.85, pred[128,2]{1,0:T(8,128)(4,1)S(1)} %copy.22), kind=kLoop, calls=%fused_computation.28 | loop fusion | flops 16777216 | bytes 67109120 | tf_op jit(solution)/shard_map/jit(_where)/select_n | solution.py:32
  47.2 11.9 %all-to-all-start = ((bf16[128,2,128,512]{3,2,1,0:T(8,128)(2,1)}), bf16[128,2,128,512]{3,2,1,0:T(8,128)(2,1)}, u32[]{:S(2)}, u32[]{:S(2)}) async-start(bf16[128,2,128,512]{3,2,1,0:T(8,128)(2,1)} %broadcast_select_fusion), calls=%async_computation | async-start | bytes 67108864 | tf_op jit(solution)/shard_map/all_to_all | solution.py:33
  63.7 478.6 %all-to-all-done = bf16[128,2,128,512]{3,2,1,0:T(8,128)(2,1)} async-done(((bf16[128,2,128,512]{3,2,1,0:T(8,128)(2,1)}), bf16[128,2,128,512]{3,2,1,0:T(8,128)(2,1)}, u32[]{:S(2)}, u32[]{:S(2)}) %all-to-all-start) | async-done | bytes 33554464 | tf_op jit(solution)/shard_map/all_to_all | solution.py:33
  542.3 25.8 %pad_maximum_fusion = bf16[288,128,512]{2,1,0:T(8,128)(2,1)} fusion(bf16[256,128,512]{2,1,0:T(8,128)(2,1)} %bitcast.19, bf16[32,128,512]{2,1,0:T(8,128)(2,1)} %bitcast.84), kind=kLoop, calls=%fused_computation.27 | loop fusion | flops 18874368 | bytes 75497472 | tf_op jit(solution)/shard_map/concatenate | solution.py:46
  570.5 112.9 %while.21 = (s32[]{:T(128)}, bf16[4,8,128,512]{3,2,1,0:T(8,128)(2,1)}, s32[4,8,16]{2,1,0:T(8,128)S(1)}, bf16[64,128,128]{2,1,0:T(8,128)(2,1)}, s32[4,8,16]{2,1,0...) while((s32[]{:T(128)}, bf16[4,8,128,512]{3,2,1,0:T(8,128)(2,1)}, s32[4,8,16]{2,1,0:T(8,128)S(1)}, ...), condition=%wide.region_4.5_spmd, body=%wide.region_3.4_spmd.sunk | while | flops 2149583616 | bytes 65027416 | solution.py:23
  575.4 13.1 %gather_fusion.2 = bf16[128,128,512]{2,1,0:T(8,128)(2,1)} fusion(bf16[288,128,512]{2,1,0:T(8,128)(2,1)} %get-tuple-element.198, s32[1024]{0:T(1024)S(1)} %pad_clamp_fusion.11), kind=kCustom, calls=%fused_computation.3.clone.1 | custom fusion | bytes 33554944 | tf_op jit(solution)/shard_map/while/body/eval_jaxpr/gather | solution.py:12
  588.4 10.4 %bitcast_dynamic-update-slice_fusion.5 = bf16[4,8,128,512]{3,2,1,0:T(8,128)(2,1)} fusion(bf16[4,8,128,512]{3,2,1,0:T(8,128)(2,1)} %get-tuple-element.187, s32[]{:T(128)} %get-tuple-element.186, bf16[8,16,128,512]{3,2,1,0:T(8,128)(2,1)} %bitcast.79, bf16[8,16,128,128]{3,2,1,0:T(8,128)(2,1)} %bitcast.81, pred[8,16]{1,0:T(8,128)(4,1)S(1)} %compare_bitcast_fusion.5), kind=kOutput, calls=%fused_computation.19.clone.1 | convolution fusion | flops 2149580800 | bytes 23069312 | tf_op jit(solution)/shard_map/while/body/eval_jaxpr/bkij,bkjn->bin/dot_general | solution.py:13
  603.7 13.2 %gather_fusion.2 = bf16[128,128,512]{2,1,0:T(8,128)(2,1)} fusion(bf16[288,128,512]{2,1,0:T(8,128)(2,1)} %get-tuple-element.198, s32[1024]{0:T(1024)S(1)} %pad_clamp_fusion.11), kind=kCustom, calls=%fused_computation.3.clone.1 | custom fusion | bytes 33554944 | tf_op jit(solution)/shard_map/while/body/eval_jaxpr/gather | solution.py:12
  616.9 10.4 %bitcast_dynamic-update-slice_fusion.5 = bf16[4,8,128,512]{3,2,1,0:T(8,128)(2,1)} fusion(bf16[4,8,128,512]{3,2,1,0:T(8,128)(2,1)} %get-tuple-element.187, s32[]{:T(128)} %get-tuple-element.186, bf16[8,16,128,512]{3,2,1,0:T(8,128)(2,1)} %bitcast.79, bf16[8,16,128,128]{3,2,1,0:T(8,128)(2,1)} %bitcast.81, pred[8,16]{1,0:T(8,128)(4,1)S(1)} %compare_bitcast_fusion.5), kind=kOutput, calls=%fused_computation.19.clone.1 | convolution fusion | flops 2149580800 | bytes 23069312 | tf_op jit(solution)/shard_map/while/body/eval_jaxpr/bkij,bkjn->bin/dot_general | solution.py:13
  632.1 13.1 %gather_fusion.2 = bf16[128,128,512]{2,1,0:T(8,128)(2,1)} fusion(bf16[288,128,512]{2,1,0:T(8,128)(2,1)} %get-tuple-element.198, s32[1024]{0:T(1024)S(1)} %pad_clamp_fusion.11), kind=kCustom, calls=%fused_computation.3.clone.1 | custom fusion | bytes 33554944 | tf_op jit(solution)/shard_map/while/body/eval_jaxpr/gather | solution.py:12
  645.2 10.4 %bitcast_dynamic-update-slice_fusion.5 = bf16[4,8,128,512]{3,2,1,0:T(8,128)(2,1)} fusion(bf16[4,8,128,512]{3,2,1,0:T(8,128)(2,1)} %get-tuple-element.187, s32[]{:T(128)} %get-tuple-element.186, bf16[8,16,128,512]{3,2,1,0:T(8,128)(2,1)} %bitcast.79, bf16[8,16,128,128]{3,2,1,0:T(8,128)(2,1)} %bitcast.81, pred[8,16]{1,0:T(8,128)(4,1)S(1)} %compare_bitcast_fusion.5), kind=kOutput, calls=%fused_computation.19.clone.1 | convolution fusion | flops 2149580800 | bytes 23069312 | tf_op jit(solution)/shard_map/while/body/eval_jaxpr/bkij,bkjn->bin/dot_general | solution.py:13
  660.5 12.6 %gather_fusion.2 = bf16[128,128,512]{2,1,0:T(8,128)(2,1)} fusion(bf16[288,128,512]{2,1,0:T(8,128)(2,1)} %get-tuple-element.198, s32[1024]{0:T(1024)S(1)} %pad_clamp_fusion.11), kind=kCustom, calls=%fused_computation.3.clone.1 | custom fusion | bytes 33554944 | tf_op jit(solution)/shard_map/while/body/eval_jaxpr/gather | solution.py:12
  673.1 10.4 %bitcast_dynamic-update-slice_fusion.5 = bf16[4,8,128,512]{3,2,1,0:T(8,128)(2,1)} fusion(bf16[4,8,128,512]{3,2,1,0:T(8,128)(2,1)} %get-tuple-element.187, s32[]{:T(128)} %get-tuple-element.186, bf16[8,16,128,512]{3,2,1,0:T(8,128)(2,1)} %bitcast.79, bf16[8,16,128,128]{3,2,1,0:T(8,128)(2,1)} %bitcast.81, pred[8,16]{1,0:T(8,128)(4,1)S(1)} %compare_bitcast_fusion.5), kind=kOutput, calls=%fused_computation.19.clone.1 | convolution fusion | flops 2149580800 | bytes 23069312 | tf_op jit(solution)/shard_map/while/body/eval_jaxpr/bkij,bkjn->bin/dot_general | solution.py:13
  685.9 107.4 %while.20 = (s32[]{:T(128)}, bf16[4,8,128,512]{3,2,1,0:T(8,128)(2,1)}, s32[4,8,16]{2,1,0:T(8,128)S(1)}, bf16[64,128,128]{2,1,0:T(8,128)(2,1)S(1)}, s32[4,8,16]{2...) while((s32[]{:T(128)}, bf16[4,8,128,512]{3,2,1,0:T(8,128)(2,1)}, s32[4,8,16]{2,1,0:T(8,128)S(1)}, ...), condition=%wide.region_1.2_spmd, body=%wide.region_0.1_spmd.sunk | while | flops 2149583616 | bytes 65027416 | solution.py:23
  689.1 13.3 %gather_fusion = bf16[128,128,512]{2,1,0:T(8,128)(2,1)} fusion(bf16[288,128,512]{2,1,0:T(8,128)(2,1)} %get-tuple-element.219, s32[1024]{0:T(1024)S(1)} %pad_clamp_fusion.9), kind=kCustom, calls=%fused_computation.1.clone.1 | custom fusion | bytes 33554944 | tf_op jit(solution)/shard_map/while/body/eval_jaxpr/gather | solution.py:12
  702.4 10.4 %bitcast_dynamic-update-slice_fusion.4 = bf16[4,8,128,512]{3,2,1,0:T(8,128)(2,1)} fusion(bf16[4,8,128,512]{3,2,1,0:T(8,128)(2,1)} %get-tuple-element.208, s32[]{:T(128)} %get-tuple-element.207, bf16[8,16,128,512]{3,2,1,0:T(8,128)(2,1)} %bitcast.80, bf16[8,16,128,128]{3,2,1,0:T(8,128)(2,1)} %bitcast.82, pred[8,16]{1,0:T(8,128)(4,1)S(1)} %compare_bitcast_fusion.4), kind=kOutput, calls=%fused_computation.8.clone.1 | convolution fusion | flops 2149580800 | bytes 23069312 | tf_op jit(solution)/shard_map/while/body/eval_jaxpr/bkij,bkjn->bin/dot_general | solution.py:13
  716.1 12.6 %gather_fusion = bf16[128,128,512]{2,1,0:T(8,128)(2,1)} fusion(bf16[288,128,512]{2,1,0:T(8,128)(2,1)} %get-tuple-element.219, s32[1024]{0:T(1024)S(1)} %pad_clamp_fusion.9), kind=kCustom, calls=%fused_computation.1.clone.1 | custom fusion | bytes 33554944 | tf_op jit(solution)/shard_map/while/body/eval_jaxpr/gather | solution.py:12
  728.6 10.5 %bitcast_dynamic-update-slice_fusion.4 = bf16[4,8,128,512]{3,2,1,0:T(8,128)(2,1)} fusion(bf16[4,8,128,512]{3,2,1,0:T(8,128)(2,1)} %get-tuple-element.208, s32[]{:T(128)} %get-tuple-element.207, bf16[8,16,128,512]{3,2,1,0:T(8,128)(2,1)} %bitcast.80, bf16[8,16,128,128]{3,2,1,0:T(8,128)(2,1)} %bitcast.82, pred[8,16]{1,0:T(8,128)(4,1)S(1)} %compare_bitcast_fusion.4), kind=kOutput, calls=%fused_computation.8.clone.1 | convolution fusion | flops 2149580800 | bytes 23069312 | tf_op jit(solution)/shard_map/while/body/eval_jaxpr/bkij,bkjn->bin/dot_general | solution.py:13
  742.4 14.1 %gather_fusion = bf16[128,128,512]{2,1,0:T(8,128)(2,1)} fusion(bf16[288,128,512]{2,1,0:T(8,128)(2,1)} %get-tuple-element.219, s32[1024]{0:T(1024)S(1)} %pad_clamp_fusion.9), kind=kCustom, calls=%fused_computation.1.clone.1 | custom fusion | bytes 33554944 | tf_op jit(solution)/shard_map/while/body/eval_jaxpr/gather | solution.py:12
  756.5 10.4 %bitcast_dynamic-update-slice_fusion.4 = bf16[4,8,128,512]{3,2,1,0:T(8,128)(2,1)} fusion(bf16[4,8,128,512]{3,2,1,0:T(8,128)(2,1)} %get-tuple-element.208, s32[]{:T(128)} %get-tuple-element.207, bf16[8,16,128,512]{3,2,1,0:T(8,128)(2,1)} %bitcast.80, bf16[8,16,128,128]{3,2,1,0:T(8,128)(2,1)} %bitcast.82, pred[8,16]{1,0:T(8,128)(4,1)S(1)} %compare_bitcast_fusion.4), kind=kOutput, calls=%fused_computation.8.clone.1 | convolution fusion | flops 2149580800 | bytes 23069312 | tf_op jit(solution)/shard_map/while/body/eval_jaxpr/bkij,bkjn->bin/dot_general | solution.py:13
  770.1 12.8 %gather_fusion = bf16[128,128,512]{2,1,0:T(8,128)(2,1)} fusion(bf16[288,128,512]{2,1,0:T(8,128)(2,1)} %get-tuple-element.219, s32[1024]{0:T(1024)S(1)} %pad_clamp_fusion.9), kind=kCustom, calls=%fused_computation.1.clone.1 | custom fusion | bytes 33554944 | tf_op jit(solution)/shard_map/while/body/eval_jaxpr/gather | solution.py:12
  782.9 10.4 %bitcast_dynamic-update-slice_fusion.4 = bf16[4,8,128,512]{3,2,1,0:T(8,128)(2,1)} fusion(bf16[4,8,128,512]{3,2,1,0:T(8,128)(2,1)} %get-tuple-element.208, s32[]{:T(128)} %get-tuple-element.207, bf16[8,16,128,512]{3,2,1,0:T(8,128)(2,1)} %bitcast.80, bf16[8,16,128,128]{3,2,1,0:T(8,128)(2,1)} %bitcast.82, pred[8,16]{1,0:T(8,128)(4,1)S(1)} %compare_bitcast_fusion.4), kind=kOutput, calls=%fused_computation.8.clone.1 | convolution fusion | flops 2149580800 | bytes 23069312 | tf_op jit(solution)/shard_map/while/body/eval_jaxpr/bkij,bkjn->bin/dot_general | solution.py:13
  803.6 200.9 %all-reduce.5.cloned.1.call-done = (f32[512,512]{0,1:T(8,128)}, f32[512,512]{0,1:T(8,128)}) async-done(((f32[512,512]{0,1:T(8,128)}, f32[512,512]{0,1:T(8,128)}), (f32[512,512]{0,1:T(8,128)}, f32[512,512]{0,1:T(8,128)})) %all-reduce.5.cloned.1.call-update) | async-done | bytes 2097168
  (95 shorter events, 55.8 us)
Async XLA Ops:
  47.2 12.2 %copy-start.2 = (s32[2,32,16]{1,2,0:T(8,128)S(1)}, s32[2,32,16]{1,2,0:T(8,128)}, u32[]{:S(2)}) copy-start(s32[2,32,16]{1,2,0:T(8,128)} %param.14) | copy-start | bytes 12292
  47.2 12.3 %copy-start.3 = (s32[2,32,16]{1,2,0:T(8,128)S(1)}, s32[2,32,16]{1,2,0:T(8,128)}, u32[]{:S(2)}) copy-start(s32[2,32,16]{1,2,0:T(8,128)} %param.13) | copy-start | bytes 12292
  47.2 495.1 %all-to-all-start = ((bf16[128,2,128,512]{3,2,1,0:T(8,128)(2,1)}), bf16[128,2,128,512]{3,2,1,0:T(8,128)(2,1)}, u32[]{:S(2)}, u32[]{:S(2)}) async-start(bf16[128,2,128,512]{3,2,1,0:T(8,128)(2,1)} %broadcast_select_fusion), calls=%async_computation | async-start | bytes 67108864 | tf_op jit(solution)/shard_map/all_to_all | solution.py:33
  59.1 945.5 %all-reduce.5.cloned.1.call-start = ((), (), s32[]{:S(2)}) async-start(), calls=%async_computation.1 | async-start | bytes 4194304
  793.3 6.9 copy-start
  793.3 6.9 copy-start.1
Sparse Core Ops, SparseCore 0:
  803.8 200.7 all-reduce.4
where the time goes:
time: 1010 us
  waiting for transfers between devices  680 us (67%)
  local copies, waits for them, and re-layouts  164 us (16%)
  matrix products  93.7 us (9%)
  other arithmetic  50.8 us (5%)
  between operations  13.5 us (1%)
  starting transfers between devices  12.1 us (1%)
    all_to_all x1, waiting for transfers between devices, fetch_blocks(): lax.all_to_all(outgoing, 'rows', split_axis=0, concat_axis=0, tiled=True)  479 us
    unnamed x2, waiting for transfers between devices  201 us
    gather x8, local copies, waits for them, and re-layouts, gather_group(): picked = source_pool[group_sources]  105 us
    dot_general x8, matrix products, gather_group(): jnp.einsum('bkij,bkjn->bin', chosen, picked, preferred_element_type=jnp.f...  83.4 us
    gather x8, local copies, waits for them, and re-layouts, gather_group(): tile_table[jnp.maximum(group_tiles, 0)]  30.7 us
    concatenate x1, other arithmetic, body(): source_pool = jnp.concatenate([blocks, arrived], axis=0)  25.8 us
    select_n x1, other arithmetic, fetch_blocks(): jnp.where(opened, blocks[jnp.maximum(send_blocks, 0)], jnp.zeros((), jnp....  22.7 us
  transfers between devices with their start and end apart: 2, of which 2 were waited for; matrix products, arithmetic and copies ran while one was open for 0% of the time, Pallas kernels for 0%

commit v1 on v0

v1 whole, which is shorter than its diff:
```python
import functools
import math

import jax
import jax.numpy as jnp
from jax import lax
from jax.experimental import pallas as pl
from jax.experimental.pallas import tpu as pltpu
from jax.sharding import PartitionSpec as P

MESH = pl.DeviceIdType.MESH
BF16, F32, I32 = jnp.bfloat16, jnp.float32, jnp.int32

STRIDE = (2, 8, 32)


def coord(me, axis):
    return (me // STRIDE[axis]) % 4


def right_mate(me, axis):
    return me + STRIDE[axis] * (1 - 2 * (coord(me, axis) % 2))


def left_mate(me, axis):
    return me + STRIDE[axis] * (3 - 2 * coord(me, axis))


def other_core(me):
    return me + 1 - 2 * (me % 2)


def cut(rows, unit):
    third = rows // unit // 3
    sizes = [rows - 2 * third * unit, third * unit, third * unit]
    starts = [0, sizes[0], sizes[0] + sizes[1]]
    return list(zip(starts, sizes))


class Cube:
    def __init__(self, own, held, parts, mates, send, recv):
        self.own, self.held, self.parts, self.mates = own, held, parts, mates
        self.send, self.recv = send, recv

    def part(self, unit, p):
        start, size = self.parts[p]
        ref = self.own if unit == 0 else self.held.at[unit]
        return ref.at[pl.ds(start, size)]

    def hop(self, p, unit, axis):
        start, size = self.parts[p]
        into = unit + (1 << axis)
        at = p * 8 + into
        return pltpu.make_async_remote_copy(
            src_ref=self.part(unit, p),
            dst_ref=self.held.at[into].at[pl.ds(start, size)],
            send_sem=self.send.at[at],
            recv_sem=self.recv.at[at],
            device_id=(self.mates[axis],),
            device_id_type=MESH,
        )

    def order(self, p):
        return [(p + n) % 3 for n in range(3)]

    def phases(self):
        result = [[] for _ in range(7)]
        for p in range(len(self.parts)):
            a, b, c = self.order(p)
            ua, ub = 1 << a, 1 << b
            for n, (unit, axis) in enumerate(
                [(0, a), (0, b), (ua, b), (0, c), (ua, c), (ub, c), (ua + ub, c)]
            ):
                result[n].append((p, unit, axis))
        return result

    def start_own(self, axis_place):
        for p in range(len(self.parts)):
            self.hop(p, 0, self.order(p)[axis_place]).start()

    def forward(self, p, unit, axis):
        got = unit + (1 << axis)
        order = self.order(p)
        for later in order[order.index(axis) + 1 :]:
            self.hop(p, got, later).start()

    def drain(self):
        for phase in self.phases():
            for hop in phase:
                self.hop(*hop).wait_send()


def gather_kernel(
    blocks, per_dir, slots,
    source_ref, tile_ref, left_ref, right_ref, block_ref, tiles_ref, need_ref, sent_ref,
    rights, lefts, needs, sents, total_ref,
    own_right, own_left, own_turned, tile_table, current, total,
    local_sem, r_send, r_recv, l_send, l_recv, n_send, n_recv, s_send, s_recv, c_send, c_recv, d_send, d_recv,
):
    me = lax.axis_index("rows")
    right_mates = [right_mate(me, axis) for axis in range(3)]
    left_mates = [left_mate(me, axis) for axis in range(3)]
    twin = other_core(me)

    barrier = pltpu.get_barrier_semaphore()
    for mate in right_mates + left_mates + [twin]:
        pl.semaphore_signal(barrier, inc=1, device_id=(mate,), device_id_type=MESH)

    left_in = pltpu.make_async_copy(left_ref, own_left, local_sem.at[0])
    left_in.start()
    right_in = pltpu.make_async_copy(block_ref, own_right, local_sem.at[1])
    right_in.start()
    tiles_in = pltpu.make_async_copy(tiles_ref, tile_table.at[pl.ds(0, tiles_ref.shape[0])], local_sem.at[2])
    tiles_in.start()
    pl.semaphore_wait(barrier, 7)

    rows = right_ref.shape[0]
    turned_rows = own_turned.shape[0]
    right_cube = Cube(right_ref, rights.at[0], cut(rows, 16), right_mates, r_send, r_recv)
    left_cube = Cube(own_turned, lefts, cut(turned_rows, 16), left_mates, l_send, l_recv)
    need_cube = Cube(need_ref, needs, [(0, need_ref.shape[0])], left_mates, n_send, n_recv)
    sent_cube = Cube(sent_ref, sents.at[0], [(0, sent_ref.shape[0])], right_mates, s_send, s_recv)

    def across(p, unit):
        start, size = right_cube.parts[p]
        at = p * 8 + unit
        return pltpu.make_async_remote_copy(
            src_ref=right_cube.part(unit, p),
            dst_ref=rights.at[1].at[unit].at[pl.ds(start, size)],
            send_sem=c_send.at[at], recv_sem=c_recv.at[at], device_id=(twin,), device_id_type=MESH,
        )

    def across_sent(unit):
        return pltpu.make_async_remote_copy(
            src_ref=sent_cube.part(unit, 0), dst_ref=sents.at[1].at[unit],
            send_sem=d_send.at[unit], recv_sem=d_recv.at[unit], device_id=(twin,), device_id_type=MESH,
        )

    for place in range(3):
        right_cube.start_own(place)
    for place in range(3):
        need_cube.start_own(place)
        sent_cube.start_own(place)
    across_sent(0).start()
    for p in range(3):
        across(p, 0).start()

    left_in.wait()
    block_rows = left_ref.shape[0] // blocks
    vectors = left_ref.shape[1]

    def turn(b, _):
        at = pl.multiple_of(b * block_rows, block_rows)
        to = pl.multiple_of(b * vectors, vectors)
        own_turned[pl.ds(to, vectors), :] = own_left[pl.ds(at, block_rows), :].T
        return 0

    lax.fori_loop(0, blocks, turn, 0)
    for place in range(3):
        left_cube.start_own(place)
    left_out = pltpu.make_async_copy(own_turned, lefts.at[0], local_sem.at[3])
    left_out.start()
    right_out = pltpu.make_async_copy(right_ref, rights.at[0].at[0], local_sem.at[4])
    right_out.start()
    need_out = pltpu.make_async_copy(need_ref, needs.at[0], local_sem.at[5])
    need_out.start()
    sent_out = pltpu.make_async_copy(sent_ref, sents.at[0].at[0], local_sem.at[6])
    sent_out.start()

    tiles_in.wait()
    right_in.wait()
    zero_tile = tiles_ref.shape[0]
    tile_table[zero_tile] = jnp.zeros(tile_table.shape[1:], BF16)
    total[...] = jnp.zeros_like(total)
    group = 8
    groups = blocks // group

    def own_group(n, _):
        d = n // groups
        first = (n % groups) * group

        def row(e, _):
            b = first + e
            summed = jnp.zeros((block_rows, vectors), F32)
            for k0 in range(0, slots, 4):
                chosen, picked = [], []
                for k in range(k0, k0 + 4):
                    chosen.append(tile_table[tile_ref[d, b, k]])
                    picked.append(own_right[source_ref[d, b, k]])
                summed = summed + jnp.dot(
                    jnp.concatenate(chosen, axis=1), jnp.concatenate(picked, axis=0), preferred_element_type=F32
                )
            current[pl.ds(pl.multiple_of(e * block_rows, block_rows), block_rows), :] = summed.astype(BF16)
            return 0

        lax.fori_loop(0, group, row, 0)
        turned = jnp.concatenate(
            [own_turned[pl.ds(pl.multiple_of((first + e) * vectors, vectors), vectors), :] for e in range(group)], axis=1
        )
        total[d] = total[d] + jnp.dot(turned, current[...], preferred_element_type=F32)
        return 0

    def compute(lo, hi):
        lax.fori_loop(lo, hi, own_group, 0)

    plan = {0: (0, 3), 1: (3, 5), 2: (5, 8)}
    phases = list(zip(right_cube.phases(), left_cube.phases()))
    small = list(zip(need_cube.phases(), sent_cube.phases()))
    for n in range(7):
        if n in plan:
            compute(*plan[n])
        if n == 3:
            total_out = pltpu.make_async_copy(total, total_ref, local_sem.at[7])
            total_out.start()
        for hop in small[n][0]:
            need_cube.hop(*hop).wait_recv()
            need_cube.forward(*hop)
        for hop in small[n][1]:
            sent_cube.hop(*hop).wait_recv()
            sent_cube.forward(*hop)
            across_sent(hop[1] + (1 << hop[2])).start()
        for hop, lhop in zip(*phases[n]):
            right_cube.hop(*hop).wait_recv()
            right_cube.forward(*hop)
            across(hop[0], hop[1] + (1 << hop[2])).start()
            left_cube.hop(*lhop).wait_recv()
            left_cube.forward(*lhop)
    for cube in (right_cube, left_cube, need_cube, sent_cube):
        cube.drain()
    for unit in range(8):
        across_sent(unit).wait()
        for p in range(3):
            across(p, unit).wait()
    for copy in (left_out, right_out, need_out, sent_out, total_out):
        copy.wait()


def gather(left, right, tiles, source_blocks, tile_index, need, sent):
    rows, vectors = right.shape
    block_rows = tiles.shape[-1]
    blocks = rows // block_rows
    table = tiles.reshape(-1, block_rows, block_rows)
    offset = jnp.arange(2, dtype=I32)[:, None, None] * tiles.shape[1]
    own = jnp.logical_and(tile_index >= 0, source_blocks < blocks)
    tile_index = jnp.where(own, tile_index + offset, table.shape[0])
    source_blocks = jnp.where(own, source_blocks, 0)
    any_spec = pl.BlockSpec(memory_space=pl.ANY)
    smem = pl.BlockSpec(memory_space=pltpu.SMEM)
    dma = pltpu.SemaphoreType.DMA
    return pl.pallas_call(
        functools.partial(gather_kernel, blocks, source_blocks.shape[1], source_blocks.shape[2]),
        out_shape=(
            jax.ShapeDtypeStruct((2, 8, rows, vectors), BF16),
            jax.ShapeDtypeStruct((8, blocks * vectors, block_rows), BF16),
            jax.ShapeDtypeStruct((8,) + need.shape, I32),
            jax.ShapeDtypeStruct((2, 8) + sent.shape, I32),
            jax.ShapeDtypeStruct((2, vectors, vectors), F32),
        ),
        in_specs=[smem, smem] + [any_spec] * 6,
        out_specs=(any_spec,) * 5,
        scratch_shapes=[
            pltpu.VMEM((blocks, block_rows, vectors), BF16),
            pltpu.VMEM((rows, vectors), BF16),
            pltpu.VMEM((blocks * vectors, block_rows), BF16),
            pltpu.VMEM((table.shape[0] + 1, block_rows, block_rows), BF16),
            pltpu.VMEM((8 * block_rows, vectors), BF16),
            pltpu.VMEM((2, vectors, vectors), F32),
            dma((8,)),
            dma((24,)), dma((24,)), dma((24,)), dma((24,)),
            dma((8,)), dma((8,)), dma((8,)), dma((8,)),
            dma((24,)), dma((24,)), dma((8,)), dma((8,)),
        ],
        compiler_params=pltpu.CompilerParams(
            collective_id=0, has_side_effects=True, vmem_limit_bytes=56 << 20
        ),
        name="gather",
    )(source_blocks, tile_index, left, right, right.reshape(blocks, block_rows, vectors), table, need, sent)


GROUP = 8
DEPTH = 3


def far_kernel(
    blocks, slots, tiles_dir,
    rights, lefts, needs, sents, tiles_ref, total_in, total_ref,
    need_s, sent_s, terms, tile_table, right_buf, left_buf, current, total, sem, rsem, lsem,
):
    me = lax.axis_index("rows")
    block_rows, vectors = right_buf.shape[-2] // GROUP, right_buf.shape[-1]
    copies = [pltpu.make_async_copy(tiles_ref, tile_table.at[pl.ds(0, tiles_ref.shape[0])], sem.at[0])]
    copies.append(pltpu.make_async_copy(total_in, total, sem.at[1]))
    for j in range(8):
        copies.append(pltpu.make_async_copy(needs.at[j, j], need_s.at[j], sem.at[2 + j]))
    for c in range(2):
        for i in range(8):
            copies.append(pltpu.make_async_copy(sents.at[c, i], sent_s.at[c * 8 + i], sem.at[10 + c * 8 + i]))
    for copy in copies:
        copy.start()
    for copy in copies[2:]:
        copy.wait()

    zero_tile = 2 * tiles_dir

    def pack(row, holder, code):
        code = jnp.maximum(code - 1, 0)
        tile = code % tiles_dir
        slot = code // tiles_dir
        at = (slot // 2, holder * 2 + slot % 2)
        block = sent_s[at[0], at[1] // 128, at[1] % 128]
        return ((row * 16 + slot // 2) * blocks + jnp.maximum(block, 0)) * tiles_dir + tile

    def list_dir(d, start):
        def unit(j, pos):
            z, x, y = coord(me, 0), coord(me, 1), coord(me, 2)
            z = jnp.where(j % 2 == 1, 3 - z, z)
            x = jnp.where((j // 2) % 2 == 1, 3 - x, x)
            y = jnp.where(j // 4 == 1, 3 - y, y)
            holder = y * STRIDE[2] + x * STRIDE[1] + z * STRIDE[0] + me % 2

            def one_row(b, pos):
                at = (d * blocks + b) * slots
                line, lane = at // 128, at % 128
                row = j * blocks + b

                def more(state):
                    k, pos = state
                    terms[pos] = pack(row, holder, need_s[j, line, lane + k])
                    return k + 1, pos + 1

                def going(state):
                    k, _ = state
                    return jnp.logical_and(k < slots, need_s[j, line, lane + jnp.minimum(k, slots - 1)] > 0)

                return lax.while_loop(going, more, (jnp.int32(0), pos))[1]

            return lax.fori_loop(0, blocks, one_row, pos)

        pos = lax.fori_loop(0, 8, unit, start)
        end = (pos + GROUP - 1) // GROUP * GROUP

        def fill(n, _):
            terms[n] = -1
            return 0

        lax.fori_loop(pos, end, fill, 0)
        return end

    half = list_dir(0, jnp.int32(0))
    end = list_dir(1, half)
    count = end // GROUP
    half = half // GROUP

    def fetch(g, e):
        word = jnp.maximum(terms[g * GROUP + e], 0)
        slot = g % DEPTH
        block = (word // tiles_dir) % blocks
        provider = (word // (tiles_dir * blocks)) % 16
        row = word // (tiles_dir * blocks * 16)
        right = pltpu.make_async_copy(
            rights.at[provider // 8, provider % 8, pl.ds(pl.multiple_of(block * block_rows, block_rows), block_rows)],
            right_buf.at[slot, pl.ds(e * block_rows, block_rows)],
            rsem.at[slot, e],
        )
        left = pltpu.make_async_copy(
            lefts.at[row // blocks, pl.ds(pl.multiple_of((row % blocks) * vectors, vectors), vectors)],
            left_buf.at[slot, e],
            lsem.at[slot, e],
        )
        return right, left

    def start(g):
        for e in range(GROUP):
            for copy in fetch(g, e):
                copy.start()

    for g in range(DEPTH - 1):
        @pl.when(g < count)
        def _():
            start(g)

    for copy in copies[:2]:
        copy.wait()
    tile_table[zero_tile] = jnp.zeros(tile_table.shape[1:], BF16)

    def step(g, _):
        @pl.when(g + DEPTH - 1 < count)
        def _():
            start(g + DEPTH - 1)

        d = jnp.where(g >= half, 1, 0)
        slot = g % DEPTH
        for e in range(GROUP):
            right, left = fetch(g, e)
            right.wait()
            left.wait()
        for e in range(GROUP):
            word = terms[g * GROUP + e]
            tile = jnp.where(word >= 0, d * tiles_dir + jnp.maximum(word, 0) % tiles_dir, zero_tile)
            current[pl.ds(e * block_rows, block_rows), :] = jnp.dot(
                tile_table[tile], right_buf[slot, pl.ds(e * block_rows, block_rows), :], preferred_element_type=F32
            ).astype(BF16)
        turned = jnp.concatenate([left_buf[slot, e] for e in range(GROUP)], axis=1)
        total[d] = total[d] + jnp.dot(turned, current[...], preferred_element_type=F32)
        return 0

    lax.fori_loop(0, count, step, 0)
    out = pltpu.make_async_copy(total, total_ref, sem.at[0])
    out.start()
    out.wait()


def far(blocks, slots, rights, lefts, needs, sents, tiles, total):
    rows, vectors = rights.shape[2:]
    block_rows = tiles.shape[-1]
    tiles_dir = tiles.shape[1]
    table = tiles.reshape(-1, block_rows, block_rows)
    any_spec = pl.BlockSpec(memory_space=pl.ANY)
    dma = pltpu.SemaphoreType.DMA
    return pl.pallas_call(
        functools.partial(far_kernel, blocks, slots, tiles_dir),
        out_shape=jax.ShapeDtypeStruct(total.shape, F32),
        in_specs=[any_spec] * 6,
        out_specs=any_spec,
        scratch_shapes=[
            pltpu.SMEM((8,) + needs.shape[2:], I32),
            pltpu.SMEM((16,) + sents.shape[2:], I32),
            pltpu.SMEM((8 * 2 * blocks * slots + 2 * GROUP,), I32),
            pltpu.VMEM((table.shape[0] + 1, block_rows, block_rows), BF16),
            pltpu.VMEM((DEPTH, GROUP * block_rows, vectors), BF16),
            pltpu.VMEM((DEPTH, GROUP, vectors, block_rows), BF16),
            pltpu.VMEM((GROUP * block_rows, vectors), BF16),
            pltpu.VMEM(total.shape, F32),
            dma((26,)), dma((DEPTH, GROUP)), dma((DEPTH, GROUP)),
        ],
        compiler_params=pltpu.CompilerParams(vmem_limit_bytes=56 << 20),
        name="far",
    )(rights, lefts, needs, sents, table, total)


def reduce_kernel(scale, total_ref, out_ref, half, sums, got_core, got_y, got_x, got_z, last, send, recv):
    me = lax.axis_index("rows")
    core = me % 2
    twin = other_core(me)

    def at(axis, n):
        c = coord(me, axis)
        return me + STRIDE[axis] * ((c + n) % 4 - c)

    peers = [twin] + [at(axis, n) for axis in range(3) for n in range(1, 4)]
    barrier = pltpu.get_barrier_semaphore()
    for peer in peers:
        pl.semaphore_signal(barrier, inc=1, device_id=(peer,), device_id_type=MESH)
    pl.semaphore_wait(barrier, len(peers))

    def copy(n, src, dst, peer):
        return pltpu.make_async_remote_copy(
            src_ref=src, dst_ref=dst, send_sem=send.at[n], recv_sem=recv.at[n], device_id=(peer,), device_id_type=MESH
        )

    swap = copy(0, total_ref.at[1 - core], got_core, twin)
    swap.start()
    swap.wait()
    half[...] = (total_ref[core] + got_core[...]) * scale

    source, size = half, half.shape[0]
    for stage, (axis, got) in enumerate(((2, got_y), (1, got_x), (0, got_z))):
        part = size // 4
        c = coord(me, axis)
        copies = []
        for n in (2, 1, 3):
            theirs = pl.multiple_of(((c + n) % 4) * part, 8)
            copies.append(copy(1 + stage * 3 + n - 1, source.at[pl.ds(theirs, part)], got.at[n - 1], at(axis, n)))
            copies[-1].start()
        for one in copies:
            one.wait()
        mine = pl.multiple_of(c * part, 8)
        into = sums.at[stage]
        into[pl.ds(0, part), :] = source[pl.ds(mine, part), :] + got[0] + got[1] + got[2]
        source, size = into, part
    give = copy(10, source.at[pl.ds(0, size)], last, twin)
    give.start()
    give.wait()
    keep = size // 2
    mine, other = source[pl.ds(0, size), :], last[...]
    first = jnp.where(core == 0, mine[:keep], other[keep:])
    second = jnp.where(core == 0, other[:keep], mine[keep:])
    out_ref[0] = first
    out_ref[1] = second


def reduce(total, scale, devices):
    _, vectors, width = total.shape
    vm = pl.BlockSpec(memory_space=pltpu.VMEM)
    return pl.pallas_call(
        functools.partial(reduce_kernel, scale),
        out_shape=jax.ShapeDtypeStruct((2, vectors // devices, width), F32),
        in_specs=[vm],
        out_specs=vm,
        scratch_shapes=[
            pltpu.VMEM((vectors, width), F32),
            pltpu.VMEM((3, vectors // 4, width), F32),
            pltpu.VMEM((vectors, width), F32),
            pltpu.VMEM((3, vectors // 4, width), F32),
            pltpu.VMEM((3, vectors // 16, width), F32),
            pltpu.VMEM((3, vectors // 64, width), F32),
            pltpu.VMEM((vectors // 64, width), F32),
            pltpu.SemaphoreType.DMA((11,)),
            pltpu.SemaphoreType.DMA((11,)),
        ],
        compiler_params=pltpu.CompilerParams(
            collective_id=1, has_side_effects=True, vmem_limit_bytes=32 << 20
        ),
        name="reduce",
    )(total)


def needs_of(source_blocks, tile_index, blocks, tiles_dir):
    me = lax.axis_index("rows")
    far_slot = jnp.maximum(source_blocks - blocks, 0)
    peer, copy = far_slot // 2, far_slot % 2
    differ = peer ^ me
    low = [(differ // STRIDE[axis]) % 2 for axis in range(3)]
    high = [(differ // (2 * STRIDE[axis])) % 2 for axis in range(3)]
    left_unit = high[0] + 2 * high[1] + 4 * high[2]
    right_unit = (low[0] ^ high[0]) + 2 * (low[1] ^ high[1]) + 4 * (low[2] ^ high[2])
    provider = (differ % 2) * 8 + right_unit
    code = (provider * 2 + copy) * tiles_dir + jnp.maximum(tile_index, 0) + 1
    live = jnp.logical_and(tile_index >= 0, source_blocks >= blocks)
    unit = jnp.where(live, left_unit, -1).reshape(-1, source_blocks.shape[-1])
    code = code.reshape(unit.shape)
    mine = unit[None] == jnp.arange(8, dtype=I32)[:, None, None]
    slots = unit.shape[-1]
    earlier = jnp.arange(slots)[:, None] < jnp.arange(slots)[None, :]
    place = jnp.sum(jnp.where(earlier[None, None], mine[..., :, None].astype(I32), 0), axis=2)
    hit = jnp.logical_and(mine[..., None, :], place[..., None, :] == jnp.arange(slots, dtype=I32)[:, None])
    packed = jnp.sum(jnp.where(hit, code[None, :, None, :], 0), axis=-1)
    return packed.reshape(8, -1, 128)


def body(left, right, tiles, source_blocks, tile_index, send_blocks):
    block_rows = tiles.shape[-1]
    rows, _ = right.shape
    blocks = rows // block_rows
    devices = lax.axis_size("rows")
    scale = 1.0 / math.sqrt(rows * devices)
    need = needs_of(source_blocks, tile_index, blocks, tiles.shape[1])
    sent = send_blocks.reshape(-1, 128)
    rights, lefts, needs, sents, total = gather(left, right, tiles, source_blocks, tile_index, need, sent)
    total = far(blocks, source_blocks.shape[2], rights, lefts, needs, sents, tiles, total)
    return reduce(total, scale, devices)


def solution(mesh):
    placed = (
        P("rows", None),
        P("rows", None),
        P(),
        P(None, "rows", None),
        P(None, "rows", None),
        P("rows", None),
    )
    return jax.shard_map(
        body, mesh=mesh, in_specs=placed, out_specs=P(None, "rows", None), check_vma=False
    )
```

time: 1010 us -> 387 us (0.38)
  waiting for transfers between devices: 680 us -> 0 us
  Pallas kernels: 0 us -> 379 us
  local copies, waits for them, and re-layouts: 164 us -> 6.26 us
  matrix products: 93.7 us -> 0 us
  other arithmetic: 50.8 us -> 1.37 us
  between operations: 13.5 us -> 0.07 us
  starting transfers between devices: 12.1 us -> 0 us
    all_to_all x1 -> x0, waiting for transfers between devices: 479 us -> none  [fetch_blocks(): lax.all_to_all(outgoing, 'rows', split_axis=0, concat_axis=0, tiled=True)]
    pallas_call x0 -> x3, Pallas kernels: none -> 379 us  [the longest x1 232 us: gather(): pl.pallas_call(functools.partial(gather_kernel, blocks, source_blocks.sha...]
    unnamed x2 -> x0, waiting for transfers between devices: 201 us -> none
    gather x17 -> x0, local copies, waits for them, and re-layouts: 152 us -> none  [the longest x8 105 us: gather_group(): picked = source_pool[group_sources]]
    dot_general x10 -> x0, matrix products: 93.7 us -> none  [the longest x8 83.4 us: gather_group(): jnp.einsum('bkij,bkjn->bin', chosen, picked, preferred_element_type=jnp.f...]
    concatenate x1 -> x0, other arithmetic: 25.8 us -> none  [body(): source_pool = jnp.concatenate([blocks, arrived], axis=0)]
    select_n x9 -> x1, other arithmetic: 22.7 us -> 0.81 us  [needs_of(): unit = jnp.where(live, left_unit, -1).reshape(-1, source_blocks.shape[-1])]
    all_to_all x1 -> x0, starting transfers between devices: 11.9 us -> none  [fetch_blocks(): lax.all_to_all(outgoing, 'rows', split_axis=0, concat_axis=0, tiled=True)]
  transfers between devices with their start and end apart: 2 -> 0, of which waited for: 2 -> 0; matrix products, arithmetic and copies ran while one was open for 0% -> 0% of each run, Pallas kernels for 0% -> 0%
where the time goes in v1:
time: 387 us; the launch traced here: 386 us
  Pallas kernels  379 us (98%)
  local copies, waits for them, and re-layouts  6.26 us (2%)
    pallas_call x1, Pallas kernels, gather(): pl.pallas_call(functools.partial(gather_kernel, blocks, source_blocks.sha...  232 us
    pallas_call x1, Pallas kernels, far(): pl.pallas_call(functools.partial(far_kernel, blocks, slots, tiles_dir), o...  91.8 us
    pallas_call x1, Pallas kernels, reduce(): pl.pallas_call(functools.partial(reduce_kernel, scale), out_shape=jax.Sha...  54.3 us

profile of v1, /device:TPU:1, one launch (start us, length us, event | category | flops | bytes accessed | tf_op | source)
XLA Modules:
  0.0 386.3 jit_solution(11334220861823176468)
XLA Ops:
  0.0 0.8 copy.24
  0.8 0.8 copy.23
  1.6 0.8 add_select_fusion.15
  2.4 0.1 copy.29
  2.5 0.1 copy.31
  2.5 0.8 copy.33
  3.3 0.7 reshape.44.sent_ref
  4.1 0.2 select_reduce_fusion.1
  4.2 0.4 select_reduce_fusion
  4.6 0.1 copy.32
  4.7 0.7 reshape.43.need_ref
  5.5 232.4 %gather.1 = (bf16[2,8,4096,512]{3,2,1,0:T(8,128)(2,1)}, bf16[8,16384,128]{2,1,0:T(8,128)(2,1)}, s32[8,8,8,128]{3,2,1,0:T(8,128)}, s32[2,8,2,128]{3,2,1,0:T(2,128)}, f32[2,512,512]{2,1,0:T(8,128)}) custom-call(s32[2,32,16]{2,1,0:T(8,128)} %get-tuple-element.17.source_ref, s32[2,32,16]{2,1,0:T(8,128)} %get-tuple-element.18.tile_ref, ...), custom_call_target="tpu_custom_call" | custom-call | tf_op jit(solution)/shard_map/gather/pallas_call | solution.py:250
  237.9 91.8 %far.1.total_ref = f32[2,512,512]{2,1,0:T(8,128)} custom-call(bf16[2,8,4096,512]{3,2,1,0:T(8,128)(2,1)} %get-tuple-element.10.rights, bf16[8,16384,128]{2,1,0:T(8,128)(2,1)} %get-tuple-element.11.lefts, s32[8,8,8,128]{3,2,1,0:T(8,128)} %get-tuple-element.12.needs, s32[2,8,2,128]{3,2,1,0:T(2,128)} %get-tuple-element.13.sents, bf16[128,128,128]{2,1,0:T(8,128)(2,1)} %bitcast.5, ...), custom_call_target="tpu_custom_call" | custom-call | tf_op jit(solution)/shard_map/far/pallas_call | solution.py:420
  329.7 0.0 copy-start
  329.8 1.6 copy-done
  331.3 54.3 %reduce.1 = f32[2,4,512]{2,1,0:T(4,128)S(1)} custom-call(f32[2,512,512]{2,1,0:T(8,128)S(1)} %copy-done), custom_call_target="tpu_custom_call" | custom-call | tf_op jit(solution)/shard_map/reduce/pallas_call | solution.py:495
  385.7 0.6 copy.35
  (3 shorter events, 0.0 us)
Async XLA Ops:
  329.7 1.6 copy-start

commit v2 on v1

--- a/solution.py
+++ b/solution.py
@@ -91,10 +91,10 @@
 
 
 def gather_kernel(
-    blocks, per_dir, slots,
-    source_ref, tile_ref, left_ref, right_ref, block_ref, tiles_ref, need_ref, sent_ref,
+    blocks, slots,
+    source_ref, tile_ref, left_ref, right_ref, block_ref, tiles_ref, info_ref, sent_ref,
     rights, lefts, needs, sents, total_ref,
-    own_right, own_left, own_turned, tile_table, current, total,
+    own_right, own_left, own_turned, tile_table, current, total, info, place_of, need_ref,
     local_sem, r_send, r_recv, l_send, l_recv, n_send, n_recv, s_send, s_recv, c_send, c_recv, d_send, d_recv,
 ):
     me = lax.axis_index("rows")
@@ -102,6 +102,8 @@
     left_mates = [left_mate(me, axis) for axis in range(3)]
     twin = other_core(me)
 
+    info_in = pltpu.make_async_copy(info_ref, info, local_sem.at[5])
+    info_in.start()
     barrier = pltpu.get_barrier_semaphore()
     for mate in right_mates + left_mates + [twin]:
         pl.semaphore_signal(barrier, inc=1, device_id=(mate,), device_id_type=MESH)
@@ -139,7 +141,6 @@
     for place in range(3):
         right_cube.start_own(place)
     for place in range(3):
-        need_cube.start_own(place)
         sent_cube.start_own(place)
     across_sent(0).start()
     for p in range(3):
@@ -162,10 +163,36 @@
     left_out.start()
     right_out = pltpu.make_async_copy(right_ref, rights.at[0].at[0], local_sem.at[4])
     right_out.start()
+    sent_out = pltpu.make_async_copy(sent_ref, sents.at[0].at[0], local_sem.at[6])
+    sent_out.start()
+
+    info_in.wait()
+    many = info.shape[1]
+    down = lax.broadcasted_iota(I32, (many, many), 0)
+    upto = jnp.where(down <= lax.broadcasted_iota(I32, (many, many), 1), 1.0, 0.0).astype(BF16)
+    eight = lax.broadcasted_iota(I32, (8, many), 0)
+    for d in range(2):
+        mine = jnp.broadcast_to(info[d : d + 1, :], (8, many)) == eight.astype(F32)
+        ranks = jnp.dot(jnp.where(mine, 1.0, 0.0).astype(BF16), upto, preferred_element_type=F32)
+        place_of[...] = jnp.where(mine, ranks, 0.0)
+        words = jnp.where(eight == 0, info[2 + d : 3 + d, :], jnp.where(eight == 1, info[4 + d : 5 + d, :], 0.0))
+        words = words.astype(BF16)
+
+        def list_for(unit, _):
+            hit = place_of[pl.ds(unit, 1), :] == (down + 1).astype(F32)
+            found = lax.dot_general(
+                words, jnp.where(hit, 1.0, 0.0).astype(BF16), (((1,), (1,)), ((), ())), preferred_element_type=F32
+            )
+            word = (found[0:1] * 256.0 + found[1:2]).astype(I32)
+            for line in range(many // 128):
+                need_ref[unit, pl.ds(d * (many // 128) + line, 1), :] = word[:, line * 128 : line * 128 + 128]
+            return 0
+
+        lax.fori_loop(0, 8, list_for, 0)
+    for place in range(3):
+        need_cube.start_own(place)
     need_out = pltpu.make_async_copy(need_ref, needs.at[0], local_sem.at[5])
     need_out.start()
-    sent_out = pltpu.make_async_copy(sent_ref, sents.at[0].at[0], local_sem.at[6])
-    sent_out.start()
 
     tiles_in.wait()
     right_in.wait()
@@ -185,8 +212,8 @@
             for k0 in range(0, slots, 4):
                 chosen, picked = [], []
                 for k in range(k0, k0 + 4):
-                    chosen.append(tile_table[tile_ref[d, b, k]])
-                    picked.append(own_right[source_ref[d, b, k]])
+                    chosen.append(tile_table[tile_ref[d, k, b]])
+                    picked.append(own_right[source_ref[d, k, b]])
                 summed = summed + jnp.dot(
                     jnp.concatenate(chosen, axis=1), jnp.concatenate(picked, axis=0), preferred_element_type=F32
                 )
@@ -235,7 +262,7 @@
         copy.wait()
 
 
-def gather(left, right, tiles, source_blocks, tile_index, need, sent):
+def gather(left, right, tiles, source_blocks, tile_index, info, sent):
     rows, vectors = right.shape
     block_rows = tiles.shape[-1]
     blocks = rows // block_rows
@@ -248,16 +275,16 @@
     smem = pl.BlockSpec(memory_space=pltpu.SMEM)
     dma = pltpu.SemaphoreType.DMA
     return pl.pallas_call(
-        functools.partial(gather_kernel, blocks, source_blocks.shape[1], source_blocks.shape[2]),
+        functools.partial(gather_kernel, blocks, source_blocks.shape[1]),
         out_shape=(
             jax.ShapeDtypeStruct((2, 8, rows, vectors), BF16),
-            jax.ShapeDtypeStruct((8, blocks * vectors, block_rows), BF16),
-            jax.ShapeDtypeStruct((8,) + need.shape, I32),
+            pltpu.VMEM((8, blocks * vectors, block_rows), BF16),
+            jax.ShapeDtypeStruct((8, 8) + (2 * info.shape[1] // 128, 128), I32),
             jax.ShapeDtypeStruct((2, 8) + sent.shape, I32),
             jax.ShapeDtypeStruct((2, vectors, vectors), F32),
         ),
         in_specs=[smem, smem] + [any_spec] * 6,
-        out_specs=(any_spec,) * 5,
+        out_specs=(any_spec, pl.BlockSpec(memory_space=pltpu.VMEM)) + (any_spec,) * 3,
         scratch_shapes=[
             pltpu.VMEM((blocks, block_rows, vectors), BF16),
             pltpu.VMEM((rows, vectors), BF16),
@@ -265,29 +292,32 @@
             pltpu.VMEM((table.shape[0] + 1, block_rows, block_rows), BF16),
             pltpu.VMEM((8 * block_rows, vectors), BF16),
             pltpu.VMEM((2, vectors, vectors), F32),
+            pltpu.VMEM(info.shape, F32),
+            pltpu.VMEM(info.shape, F32),
+            pltpu.VMEM((8, 2 * info.shape[1] // 128, 128), I32),
             dma((8,)),
             dma((24,)), dma((24,)), dma((24,)), dma((24,)),
             dma((8,)), dma((8,)), dma((8,)), dma((8,)),
             dma((24,)), dma((24,)), dma((8,)), dma((8,)),
         ],
         compiler_params=pltpu.CompilerParams(
-            collective_id=0, has_side_effects=True, vmem_limit_bytes=56 << 20
+            collective_id=0, has_side_effects=True, vmem_limit_bytes=28 << 20
         ),
         name="gather",
-    )(source_blocks, tile_index, left, right, right.reshape(blocks, block_rows, vectors), table, need, sent)
-
-
-GROUP = 8
-DEPTH = 3
+    )(source_blocks, tile_index, left, right, right.reshape(blocks, block_rows, vectors), table, info, sent)
+
+
+GROUP = 16
+DEPTH = 2
 
 
 def far_kernel(
-    blocks, slots, tiles_dir,
+    blocks, many, tiles_dir,
     rights, lefts, needs, sents, tiles_ref, total_in, total_ref,
-    need_s, sent_s, terms, tile_table, right_buf, left_buf, current, total, sem, rsem, lsem,
+    need_s, sent_s, terms, tile_table, right_buf, current, total, sem, rsem,
 ):
     me = lax.axis_index("rows")
-    block_rows, vectors = right_buf.shape[-2] // GROUP, right_buf.shape[-1]
+    block_rows, vectors = right_buf.shape[-2] // (2 * GROUP), right_buf.shape[-1]
     copies = [pltpu.make_async_copy(tiles_ref, tile_table.at[pl.ds(0, tiles_ref.shape[0])], sem.at[0])]
     copies.append(pltpu.make_async_copy(total_in, total, sem.at[1]))
     for j in range(8):
@@ -295,56 +325,59 @@
     for c in range(2):
         for i in range(8):
             copies.append(pltpu.make_async_copy(sents.at[c, i], sent_s.at[c * 8 + i], sem.at[10 + c * 8 + i]))
-    for copy in copies:
+    for copy in copies[2:] + copies[:2]:
         copy.start()
     for copy in copies[2:]:
         copy.wait()
 
     zero_tile = 2 * tiles_dir
-
-    def pack(row, holder, code):
-        code = jnp.maximum(code - 1, 0)
-        tile = code % tiles_dir
-        slot = code // tiles_dir
-        at = (slot // 2, holder * 2 + slot % 2)
-        block = sent_s[at[0], at[1] // 128, at[1] % 128]
-        return ((row * 16 + slot // 2) * blocks + jnp.maximum(block, 0)) * tiles_dir + tile
+    tile_bits = (tiles_dir - 1).bit_length()
+    block_bits = (blocks - 1).bit_length()
+    ADDR, ROW = 8, 8 + 4 + block_bits
+    UNROLL = 4
 
     def list_dir(d, start):
         def unit(j, pos):
             z, x, y = coord(me, 0), coord(me, 1), coord(me, 2)
-            z = jnp.where(j % 2 == 1, 3 - z, z)
-            x = jnp.where((j // 2) % 2 == 1, 3 - x, x)
-            y = jnp.where(j // 4 == 1, 3 - y, y)
+            z = jnp.where(j & 1 == 1, 3 - z, z)
+            x = jnp.where(j & 2 == 2, 3 - x, x)
+            y = jnp.where(j & 4 == 4, 3 - y, y)
             holder = y * STRIDE[2] + x * STRIDE[1] + z * STRIDE[0] + me % 2
-
-            def one_row(b, pos):
-                at = (d * blocks + b) * slots
-                line, lane = at // 128, at % 128
-                row = j * blocks + b
-
-                def more(state):
-                    k, pos = state
-                    terms[pos] = pack(row, holder, need_s[j, line, lane + k])
-                    return k + 1, pos + 1
-
-                def going(state):
-                    k, _ = state
-                    return jnp.logical_and(k < slots, need_s[j, line, lane + jnp.minimum(k, slots - 1)] > 0)
-
-                return lax.while_loop(going, more, (jnp.int32(0), pos))[1]
-
-            return lax.fori_loop(0, blocks, one_row, pos)
-
-        pos = lax.fori_loop(0, 8, unit, start)
-        end = (pos + GROUP - 1) // GROUP * GROUP
-
-        def fill(n, _):
-            terms[n] = -1
-            return 0
-
-        lax.fori_loop(pos, end, fill, 0)
-        return end
+            base = d * (many // 128)
+
+            def word(k):
+                return need_s[j, base + (k >> 7), k & 127]
+
+            def more(state):
+                k, pos, last, first = state
+                for u in range(UNROLL):
+                    w = word(k + u)
+                    live = jnp.minimum(w, 1)
+                    v = jnp.maximum(w - 1, 0)
+                    slot = (v >> tile_bits) & 31
+                    block = jnp.maximum(sent_s[slot >> 1, slot & 1, holder], 0)
+                    b = v >> (tile_bits + 5)
+                    address = ((slot >> 1) << block_bits) + block
+                    term = (((j << block_bits) + b) << ROW) + (address << ADDR) + d * tiles_dir + (v & (tiles_dir - 1))
+                    second = jnp.where(b == last, live, 0)
+                    first = jnp.where(second == 1, first, term)
+                    into = pos + 1 - second
+                    terms[2 * into] = first
+                    terms[2 * into + 1] = jnp.where(second == 1, term, zero_tile)
+                    pos = jnp.where(live == 1, into, pos)
+                    last = jnp.where(second == 1, -1, b)
+                return k + UNROLL, pos, last, first
+
+            def going(state):
+                k = state[0]
+                return jnp.logical_and(k < many, word(jnp.minimum(k, many - 1)) > 0)
+
+            return lax.while_loop(going, more, (jnp.int32(0), pos, jnp.int32(-1), jnp.int32(0)))[1]
+
+        pos = lax.fori_loop(0, 8, unit, start - 1) + 1
+        for u in range(2 * GROUP):
+            terms[2 * pos + u] = zero_tile
+        return (pos + GROUP - 1) // GROUP * GROUP
 
     half = list_dir(0, jnp.int32(0))
     end = list_dir(1, half)
@@ -352,28 +385,25 @@
     half = half // GROUP
 
     def fetch(g, e):
-        word = jnp.maximum(terms[g * GROUP + e], 0)
+        term = terms[g * 2 * GROUP + e]
+        address = (term >> ADDR) & ((16 << block_bits) - 1)
         slot = g % DEPTH
-        block = (word // tiles_dir) % blocks
-        provider = (word // (tiles_dir * blocks)) % 16
-        row = word // (tiles_dir * blocks * 16)
-        right = pltpu.make_async_copy(
-            rights.at[provider // 8, provider % 8, pl.ds(pl.multiple_of(block * block_rows, block_rows), block_rows)],
+        provider, block = address >> block_bits, address & (blocks - 1)
+        return term & 255 != zero_tile, pltpu.make_async_copy(
+            rights.at[provider >> 3, provider & 7, pl.ds(pl.multiple_of(block * block_rows, block_rows), block_rows)],
             right_buf.at[slot, pl.ds(e * block_rows, block_rows)],
             rsem.at[slot, e],
         )
-        left = pltpu.make_async_copy(
-            lefts.at[row // blocks, pl.ds(pl.multiple_of((row % blocks) * vectors, vectors), vectors)],
-            left_buf.at[slot, e],
-            lsem.at[slot, e],
-        )
-        return right, left
 
     def start(g):
-        for e in range(GROUP):
-            for copy in fetch(g, e):
+        for e in range(2 * GROUP):
+            needed, copy = fetch(g, e)
+
+            @pl.when(needed)
+            def _():
                 copy.start()
 
+    right_buf[...] = jnp.zeros_like(right_buf)
     for g in range(DEPTH - 1):
         @pl.when(g < count)
         def _():
@@ -390,18 +420,26 @@
 
         d = jnp.where(g >= half, 1, 0)
         slot = g % DEPTH
+        for e in range(2 * GROUP):
+            needed, copy = fetch(g, e)
+
+            @pl.when(needed)
+            def _():
+                copy.wait()
+
+        turned = []
         for e in range(GROUP):
-            right, left = fetch(g, e)
-            right.wait()
-            left.wait()
-        for e in range(GROUP):
-            word = terms[g * GROUP + e]
-            tile = jnp.where(word >= 0, d * tiles_dir + jnp.maximum(word, 0) % tiles_dir, zero_tile)
+            term, second = terms[g * 2 * GROUP + 2 * e], terms[g * 2 * GROUP + 2 * e + 1]
             current[pl.ds(e * block_rows, block_rows), :] = jnp.dot(
-                tile_table[tile], right_buf[slot, pl.ds(e * block_rows, block_rows), :], preferred_element_type=F32
+                jnp.concatenate([tile_table[term & 255], tile_table[second & 255]], axis=1),
+                right_buf[slot, pl.ds(2 * e * block_rows, 2 * block_rows), :],
+                preferred_element_type=F32,
             ).astype(BF16)
-        turned = jnp.concatenate([left_buf[slot, e] for e in range(GROUP)], axis=1)
-        total[d] = total[d] + jnp.dot(turned, current[...], preferred_element_type=F32)
+            row = term >> ROW
+            turned.append(
+                lefts[row >> block_bits, pl.ds(pl.multiple_of((row & (blocks - 1)) * vectors, vectors), vectors), :]
+            )
+        total[d] = total[d] + jnp.dot(jnp.concatenate(turned, axis=1), current[...], preferred_element_type=F32)
         return 0
 
     lax.fori_loop(0, count, step, 0)
@@ -418,27 +456,30 @@
     any_spec = pl.BlockSpec(memory_space=pl.ANY)
     dma = pltpu.SemaphoreType.DMA
     return pl.pallas_call(
-        functools.partial(far_kernel, blocks, slots, tiles_dir),
+        functools.partial(far_kernel, blocks, blocks * slots, tiles_dir),
         out_shape=jax.ShapeDtypeStruct(total.shape, F32),
-        in_specs=[any_spec] * 6,
+        in_specs=[any_spec, pl.BlockSpec(memory_space=pltpu.VMEM)] + [any_spec] * 4,
         out_specs=any_spec,
         scratch_shapes=[
             pltpu.SMEM((8,) + needs.shape[2:], I32),
             pltpu.SMEM((16,) + sents.shape[2:], I32),
-            pltpu.SMEM((8 * 2 * blocks * slots + 2 * GROUP,), I32),
+            pltpu.SMEM((2 * 8 * 2 * blocks * slots + 8 * GROUP,), I32),
             pltpu.VMEM((table.shape[0] + 1, block_rows, block_rows), BF16),
-            pltpu.VMEM((DEPTH, GROUP * block_rows, vectors), BF16),
-            pltpu.VMEM((DEPTH, GROUP, vectors, block_rows), BF16),
+            pltpu.VMEM((DEPTH, 2 * GROUP * block_rows, vectors), BF16),
             pltpu.VMEM((GROUP * block_rows, vectors), BF16),
             pltpu.VMEM(total.shape, F32),
-            dma((26,)), dma((DEPTH, GROUP)), dma((DEPTH, GROUP)),
+            dma((26,)), dma((DEPTH, 2 * GROUP)),
         ],
-        compiler_params=pltpu.CompilerParams(vmem_limit_bytes=56 << 20),
+        compiler_params=pltpu.CompilerParams(vmem_limit_bytes=28 << 20),
         name="far",
-    )(rights, lefts, needs, sents, table, total)
-
-
-def reduce_kernel(scale, total_ref, out_ref, half, sums, got_core, got_y, got_x, got_z, last, send, recv):
+    )(rights, pltpu.with_memory_space_constraint(lefts, pltpu.VMEM), needs, sents, table, total)
+
+
+LANES = ((0, 1, (1, 0, 2)), (1, 1, (0, 2, 1)), (2, 2, (2, 1, 0)))
+
+
+def reduce_kernel(scale, total_ref, out_ref, got_core, half, final, last, *rest):
+    stages, (send, recv) = rest[:-2], rest[-2:]
     me = lax.axis_index("rows")
     core = me % 2
     twin = other_core(me)
@@ -461,52 +502,70 @@
     swap = copy(0, total_ref.at[1 - core], got_core, twin)
     swap.start()
     swap.wait()
-    half[...] = (total_ref[core] + got_core[...]) * scale
-
-    source, size = half, half.shape[0]
-    for stage, (axis, got) in enumerate(((2, got_y), (1, got_x), (0, got_z))):
-        part = size // 4
-        c = coord(me, axis)
-        copies = []
-        for n in (2, 1, 3):
-            theirs = pl.multiple_of(((c + n) % 4) * part, 8)
-            copies.append(copy(1 + stage * 3 + n - 1, source.at[pl.ds(theirs, part)], got.at[n - 1], at(axis, n)))
-            copies[-1].start()
-        for one in copies:
-            one.wait()
-        mine = pl.multiple_of(c * part, 8)
-        into = sums.at[stage]
-        into[pl.ds(0, part), :] = source[pl.ds(mine, part), :] + got[0] + got[1] + got[2]
-        source, size = into, part
-    give = copy(10, source.at[pl.ds(0, size)], last, twin)
+    half[...] = ((total_ref[core] + got_core[...]) * scale).reshape(half.shape)
+
+    unit = half.shape[-1] // 4
+    everything = slice(None)
+    held = []
+    for first, lanes, order in LANES:
+        held.append(([2, 1, 0], half.at[:, :, :, :, pl.ds(first * unit, lanes * unit)]))
+    for stage in range(3):
+        started = []
+        for p, (first, lanes, order) in enumerate(LANES):
+            dims, ref = held[p]
+            axis = order[stage]
+            skip = (everything,) * dims.index(axis)
+            got = stages[2 * (3 * p + stage)]
+            for n in (2, 1, 3):
+                theirs = (coord(me, axis) + n) % 4
+                sending = copy(1 + 9 * p + 3 * stage + n - 1, ref.at[skip + (theirs,)], got.at[n - 1], at(axis, n))
+                sending.start()
+                started.append((p, sending))
+        for p, (first, lanes, order) in enumerate(LANES):
+            dims, ref = held[p]
+            axis = order[stage]
+            skip = (everything,) * dims.index(axis)
+            got, into = stages[2 * (3 * p + stage)], stages[2 * (3 * p + stage) + 1]
+            for q, sending in started:
+                if q == p:
+                    sending.wait()
+            summed = ref[skip + (coord(me, axis),)] + got[0] + got[1] + got[2]
+            if stage == 2:
+                final[:, first * unit : (first + lanes) * unit] = summed
+            else:
+                into[...] = summed
+            held[p] = ([a for a in dims if a != axis], into)
+    give = copy(28, final, last, twin)
     give.start()
     give.wait()
-    keep = size // 2
-    mine, other = source[pl.ds(0, size), :], last[...]
-    first = jnp.where(core == 0, mine[:keep], other[keep:])
-    second = jnp.where(core == 0, other[:keep], mine[keep:])
-    out_ref[0] = first
-    out_ref[1] = second
+    keep = final.shape[0] // 2
+    mine, other = final[...], last[...]
+    out_ref[0] = jnp.where(core == 0, mine[:keep], other[keep:])
+    out_ref[1] = jnp.where(core == 0, other[:keep], mine[keep:])
 
 
 def reduce(total, scale, devices):
     _, vectors, width = total.shape
+    rows = 2 * vectors // devices
     vm = pl.BlockSpec(memory_space=pltpu.VMEM)
+    stages = []
+    for _, lanes, _ in LANES:
+        for stage in range(3):
+            shape = (4,) * (2 - stage) + (rows, lanes * width // 4)
+            stages += [pltpu.VMEM((3,) + shape, F32), pltpu.VMEM(shape, F32)]
     return pl.pallas_call(
         functools.partial(reduce_kernel, scale),
-        out_shape=jax.ShapeDtypeStruct((2, vectors // devices, width), F32),
+        out_shape=jax.ShapeDtypeStruct((2, rows // 2, width), F32),
         in_specs=[vm],
         out_specs=vm,
         scratch_shapes=[
             pltpu.VMEM((vectors, width), F32),
-            pltpu.VMEM((3, vectors // 4, width), F32),
-            pltpu.VMEM((vectors, width), F32),
-            pltpu.VMEM((3, vectors // 4, width), F32),
-            pltpu.VMEM((3, vectors // 16, width), F32),
-            pltpu.VMEM((3, vectors // 64, width), F32),
-            pltpu.VMEM((vectors // 64, width), F32),
-            pltpu.SemaphoreType.DMA((11,)),
-            pltpu.SemaphoreType.DMA((11,)),
+            pltpu.VMEM((4, 4, 4, rows, width), F32),
+            pltpu.VMEM((rows, width), F32),
+            pltpu.VMEM((rows, width), F32),
+            *stages,
+            pltpu.SemaphoreType.DMA((29,)),
+            pltpu.SemaphoreType.DMA((29,)),
         ],
         compiler_params=pltpu.CompilerParams(
             collective_id=1, has_side_effects=True, vmem_limit_bytes=32 << 20
@@ -525,17 +584,12 @@
     left_unit = high[0] + 2 * high[1] + 4 * high[2]
     right_unit = (low[0] ^ high[0]) + 2 * (low[1] ^ high[1]) + 4 * (low[2] ^ high[2])
     provider = (differ % 2) * 8 + right_unit
-    code = (provider * 2 + copy) * tiles_dir + jnp.maximum(tile_index, 0) + 1
+    block = jnp.arange(blocks, dtype=I32)[None, None, :]
+    word = ((block * 16 + provider) * 2 + copy) * tiles_dir + jnp.maximum(tile_index, 0) + 1
     live = jnp.logical_and(tile_index >= 0, source_blocks >= blocks)
-    unit = jnp.where(live, left_unit, -1).reshape(-1, source_blocks.shape[-1])
-    code = code.reshape(unit.shape)
-    mine = unit[None] == jnp.arange(8, dtype=I32)[:, None, None]
-    slots = unit.shape[-1]
-    earlier = jnp.arange(slots)[:, None] < jnp.arange(slots)[None, :]
-    place = jnp.sum(jnp.where(earlier[None, None], mine[..., :, None].astype(I32), 0), axis=2)
-    hit = jnp.logical_and(mine[..., None, :], place[..., None, :] == jnp.arange(slots, dtype=I32)[:, None])
-    packed = jnp.sum(jnp.where(hit, code[None, :, None, :], 0), axis=-1)
-    return packed.reshape(8, -1, 128)
+    unit = jnp.where(live, left_unit, -1)
+    rows = jnp.stack([unit, word // 256, word % 256, jnp.zeros_like(word)])
+    return rows.astype(F32).swapaxes(2, 3).reshape(8, -1)
 
 
 def body(left, right, tiles, source_blocks, tile_index, send_blocks):
@@ -544,10 +598,11 @@
     blocks = rows // block_rows
     devices = lax.axis_size("rows")
     scale = 1.0 / math.sqrt(rows * devices)
-    need = needs_of(source_blocks, tile_index, blocks, tiles.shape[1])
-    sent = send_blocks.reshape(-1, 128)
-    rights, lefts, needs, sents, total = gather(left, right, tiles, source_blocks, tile_index, need, sent)
-    total = far(blocks, source_blocks.shape[2], rights, lefts, needs, sents, tiles, total)
+    source_blocks, tile_index = source_blocks.swapaxes(1, 2), tile_index.swapaxes(1, 2)
+    info = needs_of(source_blocks, tile_index, blocks, tiles.shape[1])
+    sent = send_blocks.T
+    rights, lefts, needs, sents, total = gather(left, right, tiles, source_blocks, tile_index, info, sent)
+    total = far(blocks, source_blocks.shape[1], rights, lefts, needs, sents, tiles, total)
     return reduce(total, scale, devices)
 
 

time: 387 us -> 326 us (0.84)
  Pallas kernels: 379 us -> 321 us
    pallas_call x1, Pallas kernels: 91.8 us -> 58.1 us  [far(): pl.pallas_call(functools.partial(far_kernel, blocks, blocks * slots, tile...]
    pallas_call x1, Pallas kernels: 54.3 us -> 27.2 us  [reduce(): pl.pallas_call(functools.partial(reduce_kernel, scale), out_shape=jax.Sha...]
where the time goes in v2:
time: 326 us; the launch traced here: 325 us
  Pallas kernels  321 us (98%)
    pallas_call x1, Pallas kernels, gather(): pl.pallas_call(functools.partial(gather_kernel, blocks, source_blocks.sha...  235 us
    pallas_call x1, Pallas kernels, far(): pl.pallas_call(functools.partial(far_kernel, blocks, blocks * slots, tile...  58.1 us
    pallas_call x1, Pallas kernels, reduce(): pl.pallas_call(functools.partial(reduce_kernel, scale), out_shape=jax.Sha...  27.2 us

profile of v2, /device:TPU:1, one launch (start us, length us, event | category | flops | bytes accessed | tf_op | source)
XLA Modules:
  0.0 325.3 jit_solution(16759925872385215001)
XLA Ops:
  0.0 0.1 pad.3.clone
  0.1 1.4 select_bitcast_fusion
  1.5 0.1 fusion
  1.6 0.1 copy.8
  1.7 0.7 reshape.22.info_ref
  2.4 235.3 %gather.1 = (bf16[2,8,4096,512]{3,2,1,0:T(8,128)(2,1)}, bf16[8,16384,128]{2,1,0:T(8,128)(2,1)S(1)}, s32[8,8,8,128]{3,2,1,0:T(8,128)}, s32[2,8,2,128]{3,2,1,0:T(2,128)}, f32[2,512,512]{2,1,0:T(8,128)}) custom-call(s32[2,16,32]{2,1,0:T(8,128)} %get-tuple-element.18.source_ref, s32[2,16,32]{2,1,0:T(8,128)} %get-tuple-element.21.tile_ref, ...), custom_call_target="tpu_custom_call" | custom-call | tf_op jit(solution)/shard_map/gather/pallas_call | solution.py:277
  237.8 58.1 %far.1.total_ref = f32[2,512,512]{2,1,0:T(8,128)} custom-call(bf16[2,8,4096,512]{3,2,1,0:T(8,128)(2,1)} %get-tuple-element.10.rights, bf16[8,16384,128]{2,1,0:T(8,128)(2,1)S(1)} %get-tuple-element.11.lefts, s32[8,8,8,128]{3,2,1,0:T(8,128)} %get-tuple-element.12.needs, s32[2,8,2,128]{3,2,1,0:T(2,128)} %get-tuple-element.13.sents, ...), custom_call_target="tpu_custom_call" | custom-call | tf_op jit(solution)/shard_map/far/pallas_call | solution.py:458
  295.9 0.0 copy-start
  295.9 1.6 copy-done
  297.5 27.2 %reduce.1 = f32[2,4,512]{2,1,0:T(4,128)S(1)} custom-call(f32[2,512,512]{2,1,0:T(8,128)S(1)} %copy-done), custom_call_target="tpu_custom_call" | custom-call | tf_op jit(solution)/shard_map/reduce/pallas_call | solution.py:556
  324.7 0.6 copy.10
  (3 shorter events, 0.0 us)
Async XLA Ops:
  295.9 1.6 copy-start

commit v3 on v2

--- a/solution.py
+++ b/solution.py
@@ -308,16 +308,16 @@
 
 
 GROUP = 16
-DEPTH = 2
+DEPTH = 4
 
 
 def far_kernel(
     blocks, many, tiles_dir,
     rights, lefts, needs, sents, tiles_ref, total_in, total_ref,
-    need_s, sent_s, terms, tile_table, right_buf, current, total, sem, rsem,
+    need_s, sent_s, terms, order, tile_table, right_buf, current, total, sem, rsem,
 ):
     me = lax.axis_index("rows")
-    block_rows, vectors = right_buf.shape[-2] // (2 * GROUP), right_buf.shape[-1]
+    block_rows, vectors = right_buf.shape[-2] // GROUP, right_buf.shape[-1]
     copies = [pltpu.make_async_copy(tiles_ref, tile_table.at[pl.ds(0, tiles_ref.shape[0])], sem.at[0])]
     copies.append(pltpu.make_async_copy(total_in, total, sem.at[1]))
     for j in range(8):
@@ -336,8 +336,13 @@
     ADDR, ROW = 8, 8 + 4 + block_bits
     UNROLL = 4
 
-    def list_dir(d, start):
-        def unit(j, pos):
+    most = 8 * many
+    single_most = 8 * blocks + 3 * GROUP
+    pair_at = [d * (most + 2 * GROUP) for d in range(2)]
+    single_at = [2 * (most + 2 * GROUP) + d * single_most for d in range(2)]
+
+    def list_dir(d):
+        def unit(j, state):
             z, x, y = coord(me, 0), coord(me, 1), coord(me, 2)
             z = jnp.where(j & 1 == 1, 3 - z, z)
             x = jnp.where(j & 2 == 2, 3 - x, x)
@@ -349,7 +354,7 @@
                 return need_s[j, base + (k >> 7), k & 127]
 
             def more(state):
-                k, pos, last, first = state
+                k, pair, single, last, first = state
                 for u in range(UNROLL):
                     w = word(k + u)
                     live = jnp.minimum(w, 1)
@@ -360,50 +365,52 @@
                     address = ((slot >> 1) << block_bits) + block
                     term = (((j << block_bits) + b) << ROW) + (address << ADDR) + d * tiles_dir + (v & (tiles_dir - 1))
                     second = jnp.where(b == last, live, 0)
-                    first = jnp.where(second == 1, first, term)
-                    into = pos + 1 - second
-                    terms[2 * into] = first
-                    terms[2 * into + 1] = jnp.where(second == 1, term, zero_tile)
-                    pos = jnp.where(live == 1, into, pos)
+                    terms[single] = term
+                    terms[pair] = first
+                    terms[pair + 1] = term
+                    pair = pair + 2 * second
+                    single = single + live - 2 * second
+                    first = term
                     last = jnp.where(second == 1, -1, b)
-                return k + UNROLL, pos, last, first
+                return k + UNROLL, pair, single, last, first
 
             def going(state):
                 k = state[0]
                 return jnp.logical_and(k < many, word(jnp.minimum(k, many - 1)) > 0)
 
-            return lax.while_loop(going, more, (jnp.int32(0), pos, jnp.int32(-1), jnp.int32(0)))[1]
-
-        pos = lax.fori_loop(0, 8, unit, start - 1) + 1
-        for u in range(2 * GROUP):
-            terms[2 * pos + u] = zero_tile
-        return (pos + GROUP - 1) // GROUP * GROUP
-
-    half = list_dir(0, jnp.int32(0))
-    end = list_dir(1, half)
-    count = end // GROUP
-    half = half // GROUP
-
-    def fetch(g, e):
-        term = terms[g * 2 * GROUP + e]
-        address = (term >> ADDR) & ((16 << block_bits) - 1)
+            return lax.while_loop(going, more, (jnp.int32(0), *state, jnp.int32(-1), jnp.int32(0)))[1:3]
+
+        ends = lax.fori_loop(0, 8, unit, (jnp.int32(pair_at[d]), jnp.int32(single_at[d])))
+        counts = []
+        for end, first in zip(ends, (pair_at[d], single_at[d])):
+            for u in range(GROUP):
+                terms[end + u] = zero_tile
+            counts.append((end - first + GROUP - 1) // GROUP)
+        return counts
+
+    count = jnp.int32(0)
+    for d in range(2):
+        for kind, (many_groups, first) in enumerate(zip(list_dir(d), (pair_at[d], single_at[d]))):
+
+            def note(n, _, kind=kind, first=first, d=d, count=count):
+                order[count + n] = ((first + n * GROUP) << 2) + d * 2 + kind
+                return 0
+
+            lax.fori_loop(0, many_groups, note, 0)
+            count = count + many_groups
+
+    def start(g):
+        at = order[g] >> 2
         slot = g % DEPTH
-        provider, block = address >> block_bits, address & (blocks - 1)
-        return term & 255 != zero_tile, pltpu.make_async_copy(
-            rights.at[provider >> 3, provider & 7, pl.ds(pl.multiple_of(block * block_rows, block_rows), block_rows)],
-            right_buf.at[slot, pl.ds(e * block_rows, block_rows)],
-            rsem.at[slot, e],
-        )
-
-    def start(g):
-        for e in range(2 * GROUP):
-            needed, copy = fetch(g, e)
-
-            @pl.when(needed)
-            def _():
-                copy.start()
-
-    right_buf[...] = jnp.zeros_like(right_buf)
+        for e in range(GROUP):
+            address = (terms[at + e] >> ADDR) & ((16 << block_bits) - 1)
+            provider, block = address >> block_bits, address & (blocks - 1)
+            pltpu.make_async_copy(
+                rights.at[provider >> 3, provider & 7, pl.ds(pl.multiple_of(block * block_rows, block_rows), block_rows)],
+                right_buf.at[slot, pl.ds(e * block_rows, block_rows)],
+                rsem.at[slot],
+            ).start()
+
     for g in range(DEPTH - 1):
         @pl.when(g < count)
         def _():
@@ -413,33 +420,38 @@
         copy.wait()
     tile_table[zero_tile] = jnp.zeros(tile_table.shape[1:], BF16)
 
+    def left_of(term):
+        row = term >> ROW
+        return lefts[row >> block_bits, pl.ds(pl.multiple_of((row & (blocks - 1)) * vectors, vectors), vectors), :]
+
     def step(g, _):
         @pl.when(g + DEPTH - 1 < count)
         def _():
             start(g + DEPTH - 1)
 
-        d = jnp.where(g >= half, 1, 0)
+        word = order[g]
+        at, d = word >> 2, (word >> 1) & 1
         slot = g % DEPTH
-        for e in range(2 * GROUP):
-            needed, copy = fetch(g, e)
-
-            @pl.when(needed)
-            def _():
-                copy.wait()
-
-        turned = []
-        for e in range(GROUP):
-            term, second = terms[g * 2 * GROUP + 2 * e], terms[g * 2 * GROUP + 2 * e + 1]
-            current[pl.ds(e * block_rows, block_rows), :] = jnp.dot(
-                jnp.concatenate([tile_table[term & 255], tile_table[second & 255]], axis=1),
-                right_buf[slot, pl.ds(2 * e * block_rows, 2 * block_rows), :],
-                preferred_element_type=F32,
-            ).astype(BF16)
-            row = term >> ROW
-            turned.append(
-                lefts[row >> block_bits, pl.ds(pl.multiple_of((row & (blocks - 1)) * vectors, vectors), vectors), :]
-            )
-        total[d] = total[d] + jnp.dot(jnp.concatenate(turned, axis=1), current[...], preferred_element_type=F32)
+        pltpu.make_async_copy(right_buf.at[slot], right_buf.at[slot], rsem.at[slot]).wait()
+        for kind, width in ((0, 2), (1, 1)):
+
+            @pl.when(word & 1 == kind)
+            def _(width=width):
+                turned = []
+                for n, e in enumerate(range(0, GROUP, width)):
+                    chosen = [tile_table[terms[at + e + u] & 255] for u in range(width)]
+                    current[pl.ds(n * block_rows, block_rows), :] = jnp.dot(
+                        jnp.concatenate(chosen, axis=1) if width > 1 else chosen[0],
+                        right_buf[slot, pl.ds(e * block_rows, width * block_rows), :],
+                        preferred_element_type=F32,
+                    ).astype(BF16)
+                    turned.append(left_of(terms[at + e]))
+                total[d] = total[d] + jnp.dot(
+                    jnp.concatenate(turned, axis=1),
+                    current[pl.ds(0, len(turned) * block_rows), :],
+                    preferred_element_type=F32,
+                )
+
         return 0
 
     lax.fori_loop(0, count, step, 0)
@@ -463,12 +475,13 @@
         scratch_shapes=[
             pltpu.SMEM((8,) + needs.shape[2:], I32),
             pltpu.SMEM((16,) + sents.shape[2:], I32),
-            pltpu.SMEM((2 * 8 * 2 * blocks * slots + 8 * GROUP,), I32),
+            pltpu.SMEM((2 * (8 * blocks * slots + 2 * GROUP + 8 * blocks + 3 * GROUP),), I32),
+            pltpu.SMEM((2 * (8 * blocks * slots + 8 * blocks) // GROUP + 8,), I32),
             pltpu.VMEM((table.shape[0] + 1, block_rows, block_rows), BF16),
-            pltpu.VMEM((DEPTH, 2 * GROUP * block_rows, vectors), BF16),
+            pltpu.VMEM((DEPTH, GROUP * block_rows, vectors), BF16),
             pltpu.VMEM((GROUP * block_rows, vectors), BF16),
             pltpu.VMEM(total.shape, F32),
-            dma((26,)), dma((DEPTH, 2 * GROUP)),
+            dma((26,)), dma((DEPTH,)),
         ],
         compiler_params=pltpu.CompilerParams(vmem_limit_bytes=28 << 20),
         name="far",
@@ -478,7 +491,7 @@
 LANES = ((0, 1, (1, 0, 2)), (1, 1, (0, 2, 1)), (2, 2, (2, 1, 0)))
 
 
-def reduce_kernel(scale, total_ref, out_ref, got_core, half, final, last, *rest):
+def reduce_kernel(scale, total_ref, out_ref, mine_core, local_sem, got_core, half, final, last, *rest):
     stages, (send, recv) = rest[:-2], rest[-2:]
     me = lax.axis_index("rows")
     core = me % 2
@@ -488,6 +501,8 @@
         c = coord(me, axis)
         return me + STRIDE[axis] * ((c + n) % 4 - c)
 
+    mine_in = pltpu.make_async_copy(total_ref.at[core], mine_core, local_sem)
+    mine_in.start()
     peers = [twin] + [at(axis, n) for axis in range(3) for n in range(1, 4)]
     barrier = pltpu.get_barrier_semaphore()
     for peer in peers:
@@ -501,8 +516,9 @@
 
     swap = copy(0, total_ref.at[1 - core], got_core, twin)
     swap.start()
+    mine_in.wait()
     swap.wait()
-    half[...] = ((total_ref[core] + got_core[...]) * scale).reshape(half.shape)
+    half[...] = ((mine_core[...] + got_core[...]) * scale).reshape(half.shape)
 
     unit = half.shape[-1] // 4
     everything = slice(None)
@@ -556,9 +572,11 @@
     return pl.pallas_call(
         functools.partial(reduce_kernel, scale),
         out_shape=jax.ShapeDtypeStruct((2, rows // 2, width), F32),
-        in_specs=[vm],
+        in_specs=[pl.BlockSpec(memory_space=pl.ANY)],
         out_specs=vm,
         scratch_shapes=[
+            pltpu.VMEM((vectors, width), F32),
+            pltpu.SemaphoreType.DMA,
             pltpu.VMEM((vectors, width), F32),
             pltpu.VMEM((4, 4, 4, rows, width), F32),
             pltpu.VMEM((rows, width), F32),
@@ -571,7 +589,7 @@
             collective_id=1, has_side_effects=True, vmem_limit_bytes=32 << 20
         ),
         name="reduce",
-    )(total)
+    )(pltpu.with_memory_space_constraint(total, pltpu.HBM))
 
 
 def needs_of(source_blocks, tile_index, blocks, tiles_dir):

time: 326 us -> 327 us (level)
    pallas_call x1, Pallas kernels: 27.2 us -> 39 us  [reduce(): pl.pallas_call(functools.partial(reduce_kernel, scale), out_shape=jax.Sha...]
    pallas_call x1, Pallas kernels: 58.1 us -> 49.2 us  [far(): pl.pallas_call(functools.partial(far_kernel, blocks, blocks * slots, tile...]
where the time goes in v3:
time: 327 us
  Pallas kernels  324 us (99%)
    pallas_call x1, Pallas kernels, gather(): pl.pallas_call(functools.partial(gather_kernel, blocks, source_blocks.sha...  235 us
    pallas_call x1, Pallas kernels, far(): pl.pallas_call(functools.partial(far_kernel, blocks, blocks * slots, tile...  49.2 us
    pallas_call x1, Pallas kernels, reduce(): pl.pallas_call(functools.partial(reduce_kernel, scale), out_shape=jax.Sha...  39 us

profile of v3, /device:TPU:1, one launch (start us, length us, event | category | flops | bytes accessed | tf_op | source)
XLA Modules:
  0.0 326.6 jit_solution(15108096135721355974)
XLA Ops:
  0.0 0.1 pad.3.clone
  0.1 1.5 select_bitcast_fusion
  1.5 0.1 fusion
  1.6 0.1 copy.8
  1.7 0.7 reshape.22.info_ref
  2.4 235.3 %gather.1 = (bf16[2,8,4096,512]{3,2,1,0:T(8,128)(2,1)}, bf16[8,16384,128]{2,1,0:T(8,128)(2,1)S(1)}, s32[8,8,8,128]{3,2,1,0:T(8,128)}, s32[2,8,2,128]{3,2,1,0:T(2,128)}, f32[2,512,512]{2,1,0:T(8,128)}) custom-call(s32[2,16,32]{2,1,0:T(8,128)} %get-tuple-element.18.source_ref, s32[2,16,32]{2,1,0:T(8,128)} %get-tuple-element.21.tile_ref, ...), custom_call_target="tpu_custom_call" | custom-call | tf_op jit(solution)/shard_map/gather/pallas_call | solution.py:277
  237.8 49.2 %far.1.total_ref = f32[2,512,512]{2,1,0:T(8,128)} custom-call(bf16[2,8,4096,512]{3,2,1,0:T(8,128)(2,1)} %get-tuple-element.10.rights, bf16[8,16384,128]{2,1,0:T(8,128)(2,1)S(1)} %get-tuple-element.11.lefts, s32[8,8,8,128]{3,2,1,0:T(8,128)} %get-tuple-element.12.needs, s32[2,8,2,128]{3,2,1,0:T(2,128)} %get-tuple-element.13.sents, ...), custom_call_target="tpu_custom_call" | custom-call | tf_op jit(solution)/shard_map/far/pallas_call | solution.py:470
  287.0 39.0 %reduce.1 = f32[2,4,512]{2,1,0:T(4,128)S(1)} custom-call(f32[2,512,512]{2,1,0:T(8,128)} %far.1.total_ref), custom_call_target="tpu_custom_call" | custom-call | tf_op jit(solution)/shard_map/reduce/pallas_call | solution.py:572
  326.0 0.6 copy.10
  (3 shorter events, 0.0 us)

commit v4 on v3

--- a/solution.py
+++ b/solution.py
@@ -388,17 +388,6 @@
             counts.append((end - first + GROUP - 1) // GROUP)
         return counts
 
-    count = jnp.int32(0)
-    for d in range(2):
-        for kind, (many_groups, first) in enumerate(zip(list_dir(d), (pair_at[d], single_at[d]))):
-
-            def note(n, _, kind=kind, first=first, d=d, count=count):
-                order[count + n] = ((first + n * GROUP) << 2) + d * 2 + kind
-                return 0
-
-            lax.fori_loop(0, many_groups, note, 0)
-            count = count + many_groups
-
     def start(g):
         at = order[g] >> 2
         slot = g % DEPTH
@@ -411,10 +400,22 @@
                 rsem.at[slot],
             ).start()
 
-    for g in range(DEPTH - 1):
-        @pl.when(g < count)
-        def _():
-            start(g)
+    count = jnp.int32(0)
+    for d in range(2):
+        begun = count
+        for kind, (many_groups, first) in enumerate(zip(list_dir(d), (pair_at[d], single_at[d]))):
+
+            def note(n, _, kind=kind, first=first, d=d, count=count):
+                order[count + n] = ((first + n * GROUP) << 2) + d * 2 + kind
+                return 0
+
+            lax.fori_loop(0, many_groups, note, 0)
+            count = count + many_groups
+        for g in range(DEPTH - 1):
+
+            @pl.when(jnp.logical_and(g >= begun, g < count))
+            def _(g=g):
+                start(g)
 
     for copy in copies[:2]:
         copy.wait()
@@ -488,7 +489,7 @@
     )(rights, pltpu.with_memory_space_constraint(lefts, pltpu.VMEM), needs, sents, table, total)
 
 
-LANES = ((0, 1, (1, 0, 2)), (1, 1, (0, 2, 1)), (2, 2, (2, 1, 0)))
+LANES = ((2, 2, (2, 1, 0)), (0, 1, (1, 0, 2)), (1, 1, (0, 2, 1)))
 
 
 def reduce_kernel(scale, total_ref, out_ref, mine_core, local_sem, got_core, half, final, last, *rest):
@@ -514,13 +515,16 @@
             src_ref=src, dst_ref=dst, send_sem=send.at[n], recv_sem=recv.at[n], device_id=(peer,), device_id_type=MESH
         )
 
-    swap = copy(0, total_ref.at[1 - core], got_core, twin)
-    swap.start()
+    unit = got_core.shape[-1] // 4
+    swaps = []
+    for p, (first, lanes, order) in enumerate(LANES):
+        columns = pl.ds(first * unit, lanes * unit)
+        swaps.append(
+            copy(28 + p, total_ref.at[1 - core].at[:, columns], got_core.at[:, columns], twin)
+        )
+        swaps[-1].start()
     mine_in.wait()
-    swap.wait()
-    half[...] = ((mine_core[...] + got_core[...]) * scale).reshape(half.shape)
-
-    unit = half.shape[-1] // 4
+
     everything = slice(None)
     held = []
     for first, lanes, order in LANES:
@@ -532,6 +536,11 @@
             axis = order[stage]
             skip = (everything,) * dims.index(axis)
             got = stages[2 * (3 * p + stage)]
+            if stage == 0:
+                swaps[p].wait()
+                columns = slice(first * unit, (first + lanes) * unit)
+                both = (mine_core[:, columns] + got_core[:, columns]) * scale
+                half[:, :, :, :, columns] = both.reshape(half.shape[:-1] + (lanes * unit,))
             for n in (2, 1, 3):
                 theirs = (coord(me, axis) + n) % 4
                 sending = copy(1 + 9 * p + 3 * stage + n - 1, ref.at[skip + (theirs,)], got.at[n - 1], at(axis, n))
@@ -551,7 +560,7 @@
             else:
                 into[...] = summed
             held[p] = ([a for a in dims if a != axis], into)
-    give = copy(28, final, last, twin)
+    give = copy(0, final, last, twin)
     give.start()
     give.wait()
     keep = final.shape[0] // 2
@@ -582,8 +591,8 @@
             pltpu.VMEM((rows, width), F32),
             pltpu.VMEM((rows, width), F32),
             *stages,
-            pltpu.SemaphoreType.DMA((29,)),
-            pltpu.SemaphoreType.DMA((29,)),
+            pltpu.SemaphoreType.DMA((31,)),
+            pltpu.SemaphoreType.DMA((31,)),
         ],
         compiler_params=pltpu.CompilerParams(
             collective_id=1, has_side_effects=True, vmem_limit_bytes=32 << 20

time: 327 us -> 322 us (0.985)
  Pallas kernels: 324 us -> 318 us
    pallas_call x1, Pallas kernels: 39 us -> 30.2 us  [reduce(): pl.pallas_call(functools.partial(reduce_kernel, scale), out_shape=jax.Sha...]
where the time goes in v4:
time: 322 us; the launch traced here: 321 us
  Pallas kernels  318 us (99%)
    pallas_call x1, Pallas kernels, gather(): pl.pallas_call(functools.partial(gather_kernel, blocks, source_blocks.sha...  235 us
    pallas_call x1, Pallas kernels, far(): pl.pallas_call(functools.partial(far_kernel, blocks, blocks * slots, tile...  52 us
    pallas_call x1, Pallas kernels, reduce(): pl.pallas_call(functools.partial(reduce_kernel, scale), out_shape=jax.Sha...  30.2 us

profile of v4, /device:TPU:1, one launch (start us, length us, event | category | flops | bytes accessed | tf_op | source)
XLA Modules:
  0.0 320.6 jit_solution(7221550079833277990)
XLA Ops:
  0.0 0.1 pad.3.clone
  0.1 1.5 select_bitcast_fusion
  1.5 0.1 fusion
  1.6 0.1 copy.8
  1.7 0.7 reshape.22.info_ref
  2.4 235.3 %gather.1 = (bf16[2,8,4096,512]{3,2,1,0:T(8,128)(2,1)}, bf16[8,16384,128]{2,1,0:T(8,128)(2,1)S(1)}, s32[8,8,8,128]{3,2,1,0:T(8,128)}, s32[2,8,2,128]{3,2,1,0:T(2,128)}, f32[2,512,512]{2,1,0:T(8,128)}) custom-call(s32[2,16,32]{2,1,0:T(8,128)} %get-tuple-element.18.source_ref, s32[2,16,32]{2,1,0:T(8,128)} %get-tuple-element.21.tile_ref, ...), custom_call_target="tpu_custom_call" | custom-call | tf_op jit(solution)/shard_map/gather/pallas_call | solution.py:277
  237.8 52.0 %far.1.total_ref = f32[2,512,512]{2,1,0:T(8,128)} custom-call(bf16[2,8,4096,512]{3,2,1,0:T(8,128)(2,1)} %get-tuple-element.10.rights, bf16[8,16384,128]{2,1,0:T(8,128)(2,1)S(1)} %get-tuple-element.11.lefts, s32[8,8,8,128]{3,2,1,0:T(8,128)} %get-tuple-element.12.needs, s32[2,8,2,128]{3,2,1,0:T(2,128)} %get-tuple-element.13.sents, ...), custom_call_target="tpu_custom_call" | custom-call | tf_op jit(solution)/shard_map/far/pallas_call | solution.py:471
  289.8 30.2 %reduce.1 = f32[2,4,512]{2,1,0:T(4,128)S(1)} custom-call(f32[2,512,512]{2,1,0:T(8,128)} %far.1.total_ref), custom_call_target="tpu_custom_call" | custom-call | tf_op jit(solution)/shard_map/reduce/pallas_call | solution.py:581
  320.0 0.6 copy.10
  (3 shorter events, 0.0 us)

commit v5 on v4

--- a/solution.py
+++ b/solution.py
@@ -322,9 +322,7 @@
     copies.append(pltpu.make_async_copy(total_in, total, sem.at[1]))
     for j in range(8):
         copies.append(pltpu.make_async_copy(needs.at[j, j], need_s.at[j], sem.at[2 + j]))
-    for c in range(2):
-        for i in range(8):
-            copies.append(pltpu.make_async_copy(sents.at[c, i], sent_s.at[c * 8 + i], sem.at[10 + c * 8 + i]))
+    copies.append(pltpu.make_async_copy(sents, sent_s, sem.at[10]))
     for copy in copies[2:] + copies[:2]:
         copy.start()
     for copy in copies[2:]:
@@ -334,7 +332,7 @@
     tile_bits = (tiles_dir - 1).bit_length()
     block_bits = (blocks - 1).bit_length()
     ADDR, ROW = 8, 8 + 4 + block_bits
-    UNROLL = 4
+    UNROLL = 8
 
     most = 8 * many
     single_most = 8 * blocks + 3 * GROUP
@@ -360,7 +358,7 @@
                     live = jnp.minimum(w, 1)
                     v = jnp.maximum(w - 1, 0)
                     slot = (v >> tile_bits) & 31
-                    block = jnp.maximum(sent_s[slot >> 1, slot & 1, holder], 0)
+                    block = jnp.maximum(sent_s[slot >> 4, (slot >> 1) & 7, slot & 1, holder], 0)
                     b = v >> (tile_bits + 5)
                     address = ((slot >> 1) << block_bits) + block
                     term = (((j << block_bits) + b) << ROW) + (address << ADDR) + d * tiles_dir + (v & (tiles_dir - 1))
@@ -475,7 +473,7 @@
         out_specs=any_spec,
         scratch_shapes=[
             pltpu.SMEM((8,) + needs.shape[2:], I32),
-            pltpu.SMEM((16,) + sents.shape[2:], I32),
+            pltpu.SMEM(sents.shape, I32),
             pltpu.SMEM((2 * (8 * blocks * slots + 2 * GROUP + 8 * blocks + 3 * GROUP),), I32),
             pltpu.SMEM((2 * (8 * blocks * slots + 8 * blocks) // GROUP + 8,), I32),
             pltpu.VMEM((table.shape[0] + 1, block_rows, block_rows), BF16),

time: 322 us -> 324 us (level)
  Pallas kernels: 318 us -> 322 us
    pallas_call x1, Pallas kernels: 30.2 us -> 34.6 us  [reduce(): pl.pallas_call(functools.partial(reduce_kernel, scale), out_shape=jax.Sha...]
where the time goes in v5:
time: 324 us; the launch traced here: 325 us
  Pallas kernels  322 us (99%)
    pallas_call x1, Pallas kernels, gather(): pl.pallas_call(functools.partial(gather_kernel, blocks, source_blocks.sha...  235 us
    pallas_call x1, Pallas kernels, far(): pl.pallas_call(functools.partial(far_kernel, blocks, blocks * slots, tile...  51.7 us
    pallas_call x1, Pallas kernels, reduce(): pl.pallas_call(functools.partial(reduce_kernel, scale), out_shape=jax.Sha...  34.6 us

profile of v5, /device:TPU:1, one launch (start us, length us, event | category | flops | bytes accessed | tf_op | source)
XLA Modules:
  0.0 324.7 jit_solution(1537880516822073222)
XLA Ops:
  0.0 0.1 pad.3.clone
  0.1 1.5 select_bitcast_fusion
  1.5 0.1 fusion
  1.6 0.1 copy.8
  1.7 0.7 reshape.22.info_ref
  2.4 235.3 %gather.1 = (bf16[2,8,4096,512]{3,2,1,0:T(8,128)(2,1)}, bf16[8,16384,128]{2,1,0:T(8,128)(2,1)S(1)}, s32[8,8,8,128]{3,2,1,0:T(8,128)}, s32[2,8,2,128]{3,2,1,0:T(2,128)}, f32[2,512,512]{2,1,0:T(8,128)}) custom-call(s32[2,16,32]{2,1,0:T(8,128)} %get-tuple-element.18.source_ref, s32[2,16,32]{2,1,0:T(8,128)} %get-tuple-element.21.tile_ref, ...), custom_call_target="tpu_custom_call" | custom-call | tf_op jit(solution)/shard_map/gather/pallas_call | solution.py:277
  237.8 51.7 %far.1.total_ref = f32[2,512,512]{2,1,0:T(8,128)} custom-call(bf16[2,8,4096,512]{3,2,1,0:T(8,128)(2,1)} %get-tuple-element.10.rights, bf16[8,16384,128]{2,1,0:T(8,128)(2,1)S(1)} %get-tuple-element.11.lefts, s32[8,8,8,128]{3,2,1,0:T(8,128)} %get-tuple-element.12.needs, s32[2,8,2,128]{3,2,1,0:T(2,128)} %get-tuple-element.13.sents, ...), custom_call_target="tpu_custom_call" | custom-call | tf_op jit(solution)/shard_map/far/pallas_call | solution.py:469
  289.5 34.6 %reduce.1 = f32[2,4,512]{2,1,0:T(4,128)S(1)} custom-call(f32[2,512,512]{2,1,0:T(8,128)} %far.1.total_ref), custom_call_target="tpu_custom_call" | custom-call | tf_op jit(solution)/shard_map/reduce/pallas_call | solution.py:579
  324.1 0.6 copy.10
  (3 shorter events, 0.0 us)
